TPU v7x, 32 devices: a whole 2x2x4 slice. The times are simulated.
32 devices in a mesh: groups: 2 (over y), segment: 4 (over z), inner: 4 (over x, core).
Axes of the slice: x: 2, y: 2, z: 4, core: 2. Of those that a mesh axis runs over, the one named last changes fastest.
Arguments:
- tokens: int32 [3, 64], P(None, 'groups'), parts along dimension 1, may hold values from 0 to 511
- embedding: bfloat16 [512, 4096], P(None, 'inner'), may hold values from -6 to 6
- in_proj: bfloat16 [4, 3, 4096, 4096], P('segment', None, None, 'inner'), may hold values from -0.09375 to 0.09375
- out_proj: bfloat16 [4, 4096, 4096], P('segment', 'inner'), may hold values from -0.09375 to 0.09375
- norm_gain: float32 [4, 4096], P('segment'), may hold values from 0.1 to 1.9
- fir_taps: float32 [4, 7, 4096], P('segment', None, 'inner'), may hold values from -2 to 2
- modal_rate: float32 [4, 8, 4096], P('segment', None, 'inner'), may hold values from 0.05 to 3
- modal_residue: float32 [4, 8, 4096], P('segment', None, 'inner'), may hold values from -2 to 2
- fir_state: float32 [4, 64, 6, 4096], P('segment', 'groups', None, 'inner'), parts along dimension 1, may hold values from -6 to 6
- modal_state: float32 [4, 64, 8, 4096], P('segment', 'groups', None, 'inner'), parts along dimension 1, may hold values from -6 to 6
- final_gain: float32 [4096], replicated, may hold values from 0.1 to 1.9
- unembed: bfloat16 [4096, 512], P(None, 'inner'), may hold values from -0.25 to 0.25
Outputs:
- logits: float32 [2, 64, 512], P(None, ('groups', 'segment'), 'inner'), parts along dimension 1
- logprob: float32 [2, 64], P(None, ('groups', 'segment')), parts along dimension 1
- fir_state_out: float32 [4, 64, 6, 4096], P('segment', 'groups', None, 'inner'), parts along dimension 1
- modal_state_out: float32 [4, 64, 8, 4096], P('segment', 'groups', None, 'inner'), parts along dimension 1
There are 2 independent parts, one for each index of `groups`. A program takes and returns all parts, laid end to end along the dimension named above; an argument that names none is the same for every part. Nothing has to cross between parts.
All inputs are finite; a program needn't handle non-finite values.
Results may differ from a plain program's by a relative error of at most 0.025.
Values may be sent and summed in bfloat16 or wider, within the bound.
No kernel may reach another device: no remote copies, remote signals or barrier semaphores. Data moves between devices by JAX's collectives and lax.ppermute only.
A program may use at most 128 MiB of HBM per device.

v0:
```python
import jax
import jax.numpy as jnp
from jax import lax
from jax.sharding import PartitionSpec as P

MICRO = 2


def from_behind(block, axis, distance):
    devices = range(lax.axis_size(axis))
    route = [(i - distance, i) for i in devices if i - distance in devices]
    return lax.ppermute(block, axis, route)


def normed(values, scale_gain):
    mean_square = jnp.mean(values * values, axis=-1, keepdims=True)
    return values * lax.rsqrt(mean_square + 1e-05) * scale_gain


def short_filter(operands):
    product, fir_rows, modal_rows, taps_local, rate_local, residue_local = operands
    window = jnp.concatenate([fir_rows, product[:, None, :]], axis=1)
    filtered = jnp.sum(window * taps_local[::-1][None], axis=1)
    return (filtered, window[:, 1:], modal_rows)


def modal_filter(operands):
    product, fir_rows, modal_rows, taps_local, rate_local, residue_local = operands
    decay_factor = jnp.exp(-rate_local)
    mode_values = decay_factor[None] * modal_rows + (1.0 - decay_factor[None]) * product[:, None, :]
    filtered = jnp.sum(residue_local[None] * mode_values, axis=1) + taps_local[0][None] * product
    return (filtered, fir_rows, mode_values)


def per_device(
    tokens,
    embedding,
    in_proj,
    out_proj,
    norm_gain,
    fir_taps,
    modal_rate,
    modal_residue,
    fir_state,
    modal_state,
    final_gain,
    unembed,
):
    segment_count = lax.axis_size("segment")
    segment_index = lax.axis_index("segment")
    inner_index = lax.axis_index("inner")
    step_count = tokens.shape[0] - 1
    seq_count = tokens.shape[1]
    block_count = MICRO
    row_count = seq_count // block_count
    item_count = step_count * block_count
    tick_count = item_count + segment_count - 1
    local_width = embedding.shape[1]
    w_in = in_proj[0]
    w_out = out_proj[0]
    gain_local = norm_gain[0]
    taps_local = fir_taps[0]
    rate_local = modal_rate[0]
    residue_local = modal_residue[0]
    is_short = segment_index % 2 == 0
    is_last = segment_index == segment_count - 1

    def advance(carry, tick_index):
        previous, fir_all, modal_all, recorded = carry
        item_index = tick_index - segment_index
        is_valid = (item_index >= 0) & (item_index < item_count)
        clipped = jnp.clip(item_index, 0, item_count - 1)
        step_index = clipped // block_count
        row_start = clipped % block_count * row_count
        incoming = from_behind(previous, "segment", 1)
        token_ids = lax.dynamic_slice(tokens, (step_index, row_start), (1, row_count))[0]
        looked_up = jnp.take(embedding, token_ids, axis=0)
        stream_in = jnp.where(segment_index == 0, looked_up, incoming)
        gathered = lax.all_gather(stream_in, "inner", axis=1, tiled=True)
        normalized = normed(gathered.astype(jnp.float32), gain_local).astype(jnp.bfloat16)
        projected = jnp.einsum("bd,jdc->jbc", normalized, w_in, preferred_element_type=jnp.float32)
        product = projected[1] * projected[2]
        fir_rows = lax.dynamic_slice_in_dim(fir_all, row_start, row_count, 0)
        modal_rows = lax.dynamic_slice_in_dim(modal_all, row_start, row_count, 0)
        filtered, fir_next, modal_next = lax.cond(
            is_short,
            short_filter,
            modal_filter,
            (product, fir_rows, modal_rows, taps_local, rate_local, residue_local),
        )
        fir_all = lax.dynamic_update_slice_in_dim(
            fir_all, jnp.where(is_valid, fir_next, fir_rows), row_start, 0
        )
        modal_all = lax.dynamic_update_slice_in_dim(
            modal_all, jnp.where(is_valid, modal_next, modal_rows), row_start, 0
        )
        gated_rows = (projected[0] * filtered).astype(jnp.bfloat16)
        partial_sum = jnp.dot(gated_rows, w_out, preferred_element_type=jnp.float32)
        mixed_sum = lax.psum_scatter(partial_sum, "inner", scatter_dimension=1, tiled=True)
        stream_out = (stream_in.astype(jnp.float32) + mixed_sum).astype(jnp.bfloat16)
        current = lax.dynamic_slice(
            recorded, (step_index, row_start, jnp.int32(0)), (1, row_count, local_width)
        )
        recorded = lax.dynamic_update_slice(
            recorded,
            jnp.where(is_valid & is_last, stream_out[None], current),
            (step_index, row_start, jnp.int32(0)),
        )
        return ((stream_out, fir_all, modal_all, recorded), None)

    initial = (
        jnp.zeros((row_count, local_width), jnp.bfloat16),
        fir_state[0],
        modal_state[0],
        jnp.zeros((step_count, seq_count, local_width), jnp.bfloat16),
    )
    final_carry, unused = lax.scan(advance, initial, jnp.arange(tick_count, dtype=jnp.int32))
    last_out, fir_final, modal_final, recorded = final_carry
    final_stream = lax.all_gather(recorded, "inner", axis=2, tiled=True)
    head_in = normed(final_stream.astype(jnp.float32), final_gain).astype(jnp.bfloat16)
    logits = jnp.einsum("tsd,dv->tsv", head_in, unembed, preferred_element_type=jnp.float32)
    vocab_local = unembed.shape[1]
    columns = inner_index * vocab_local + jnp.arange(vocab_local, dtype=jnp.int32)
    targets = tokens[1:]
    exp_local = jnp.sum(jnp.exp(logits), axis=-1)
    target_part = jnp.sum(
        jnp.where(columns[None, None, :] == targets[:, :, None], logits, 0.0), axis=-1
    )
    exp_total, target_logit = lax.psum((exp_local, target_part), "inner")
    logprob = target_logit - jnp.log(exp_total)
    logits_kept = jnp.where(is_last, logits, 0.0)
    logprob_kept = jnp.where(is_last, logprob, 0.0)
    logits_out, logprob_out = (
        lax.psum_scatter(logits_kept, "segment", scatter_dimension=1, tiled=True),
        lax.psum_scatter(logprob_kept, "segment", scatter_dimension=1, tiled=True),
    )
    return (logits_out, logprob_out, fir_final[None], modal_final[None])


def solution(mesh):
    return jax.shard_map(
        per_device,
        mesh=mesh,
        in_specs=(
            P(None, "groups"),
            P(None, "inner"),
            P("segment", None, None, "inner"),
            P("segment", "inner", None),
            P("segment", None),
            P("segment", None, "inner"),
            P("segment", None, "inner"),
            P("segment", None, "inner"),
            P("segment", "groups", None, "inner"),
            P("segment", "groups", None, "inner"),
            P(),
            P(None, "inner"),
        ),
        out_specs=(
            P(None, ("groups", "segment"), "inner"),
            P(None, ("groups", "segment")),
            P("segment", "groups", None, "inner"),
            P("segment", "groups", None, "inner"),
        ),
        check_vma=False,
    )
```

profile of v0, /device:TPU:0, one launch (start us, length us, event | category | flops | bytes accessed | tf_op | source)
XLA Modules:
  0.0 421.6 jit_solution(7223854443020577943)
XLA Ops:
  8.0 2.4 copy.56
  10.4 2.6 copy.26
  14.5 369.0 %while.19 = (s32[]{:T(128)}, bf16[16,1024]{1,0:T(8,128)(2,1)S(1)}, f32[32,6,1024]{2,1,0:T(8,128)}, f32[32,8,1024]{2,1,0:T(8,128)}, bf16[2,32,1024]{2,1,0:T(8,128...) while((s32[]{:T(128)}, bf16[16,1024]{1,0:T(8,128)(2,1)S(1)}, ...), condition=%wide.region_7.8_spmd.clone, body=%wide.region_0.7_spmd.clone.sunk | while | flops 538412224 | bytes 43820432 | solution.py:117
  14.6 5.0 %collective-permute-start = (bf16[16,1024]{1,0:T(8,128)(2,1)S(1)}, bf16[16,1024]{1,0:T(8,128)(2,1)S(1)}, u32[]{:S(2)}, u32[]{:S(2)}) collective-permute-start(bf16[16,1024]{1,0:T(8,128)(2,1)S(1)} %broadcast_select_fusion.3), channel_id=1, source_target_pairs={{0,4},{4,8},{8,12},{1,5},{5,9},{9,13},{2,6},{6,10},{10,14},{3,7},{... | collective-permute-start | bytes 98312 | tf_op jit(solution)/shard_map/while/body/eval_jaxpr/ppermute | solution.py:12
  24.5 2.0 gather_fusion
  26.6 5.4 %all_gather.12 = bf16[16,4096]{1,0:T(8,128)(2,1)S(1)} all-gather(bf16[16,1024]{1,0:T(8,128)(2,1)S(1)} %select_select_fusion.2), channel_id=1, replica_groups=mesh['groups'=2,'segment'=4,'inner'=4] {'inner'}, dimensions={1}, use_global_device_ids=true | all-gather | bytes 163840 | tf_op jit(solution)/shard_map/while/body/eval_jaxpr/all_gather | solution.py:79
  32.2 10.0 %convolution_bitcast_fusion.2 = f32[3,16,1024]{2,1,0:T(8,128)S(1)} fusion(bf16[3,4096,1024]{2,1,0:T(8,128)(2,1)} %get-tuple-element.555, bf16[16,4096]{1,0:T(8,128)(2,1)S(1)} %all_gather.12, f32[4096]{0:T(1024)} %bitcast.78, f32[16]{0:T(128)S(1)} %add_rsqrt_fusion.3), kind=kOutput, calls=%fused_computation.11.clone.1 | convolution fusion | flops 402915328 | bytes 25509952 | tf_op jit(solution)/shard_map/while/body/eval_jaxpr/bd,jdc->jbc/dot_general | solution.py:81
  42.9 5.3 %fusion.43 = f32[16,4096]{1,0:T(8,128)} fusion(bf16[1024,4096]{1,0:T(8,128)(2,1)} %get-tuple-element.560, f32[16,1024]{1,0:T(8,128)S(1)} %get-tuple-element.481, f32[3,16,1024]{2,1,0:T(8,128)S(1)} %convolution_bitcast_fusion.2), kind=kOutput, calls=%fused_computation.28.clone.1 | convolution fusion | flops 134250496 | bytes 8781824 | tf_op jit(solution)/shard_map/while/body/eval_jaxpr/dot_general | solution.py:98
  52.0 16.6 %reduce-scatter.6.cloned.1.call-done = f32[16,1024]{1,0:T(8,128)} async-done(((f32[16,4096]{1,0:T(8,128)}), f32[16,1024]{1,0:T(8,128)}) %reduce-scatter.6.cloned.1.call-update) | async-done | bytes 65552 | tf_op jit(solution)/shard_map/while/body/eval_jaxpr/reduce_scatter | solution.py:99
  69.6 3.4 collective-permute-start
  78.0 2.0 gather_fusion
  80.1 5.4 %all_gather.12 = bf16[16,4096]{1,0:T(8,128)(2,1)S(1)} all-gather(bf16[16,1024]{1,0:T(8,128)(2,1)S(1)} %select_select_fusion.2), channel_id=1, replica_groups=mesh['groups'=2,'segment'=4,'inner'=4] {'inner'}, dimensions={1}, use_global_device_ids=true | all-gather | bytes 163840 | tf_op jit(solution)/shard_map/while/body/eval_jaxpr/all_gather | solution.py:79
  85.6 10.0 %convolution_bitcast_fusion.2 = f32[3,16,1024]{2,1,0:T(8,128)S(1)} fusion(bf16[3,4096,1024]{2,1,0:T(8,128)(2,1)} %get-tuple-element.555, bf16[16,4096]{1,0:T(8,128)(2,1)S(1)} %all_gather.12, f32[4096]{0:T(1024)} %bitcast.78, f32[16]{0:T(128)S(1)} %add_rsqrt_fusion.3), kind=kOutput, calls=%fused_computation.11.clone.1 | convolution fusion | flops 402915328 | bytes 25509952 | tf_op jit(solution)/shard_map/while/body/eval_jaxpr/bd,jdc->jbc/dot_general | solution.py:81
  96.4 5.3 %fusion.43 = f32[16,4096]{1,0:T(8,128)} fusion(bf16[1024,4096]{1,0:T(8,128)(2,1)} %get-tuple-element.560, f32[16,1024]{1,0:T(8,128)S(1)} %get-tuple-element.481, f32[3,16,1024]{2,1,0:T(8,128)S(1)} %convolution_bitcast_fusion.2), kind=kOutput, calls=%fused_computation.28.clone.1 | convolution fusion | flops 134250496 | bytes 8781824 | tf_op jit(solution)/shard_map/while/body/eval_jaxpr/dot_general | solution.py:98
  105.5 15.5 %reduce-scatter.6.cloned.1.call-done = f32[16,1024]{1,0:T(8,128)} async-done(((f32[16,4096]{1,0:T(8,128)}), f32[16,1024]{1,0:T(8,128)}) %reduce-scatter.6.cloned.1.call-update) | async-done | bytes 65552 | tf_op jit(solution)/shard_map/while/body/eval_jaxpr/reduce_scatter | solution.py:99
  121.9 3.4 collective-permute-start
  130.3 2.0 gather_fusion
  132.4 5.4 %all_gather.12 = bf16[16,4096]{1,0:T(8,128)(2,1)S(1)} all-gather(bf16[16,1024]{1,0:T(8,128)(2,1)S(1)} %select_select_fusion.2), channel_id=1, replica_groups=mesh['groups'=2,'segment'=4,'inner'=4] {'inner'}, dimensions={1}, use_global_device_ids=true | all-gather | bytes 163840 | tf_op jit(solution)/shard_map/while/body/eval_jaxpr/all_gather | solution.py:79
  138.0 10.0 %convolution_bitcast_fusion.2 = f32[3,16,1024]{2,1,0:T(8,128)S(1)} fusion(bf16[3,4096,1024]{2,1,0:T(8,128)(2,1)} %get-tuple-element.555, bf16[16,4096]{1,0:T(8,128)(2,1)S(1)} %all_gather.12, f32[4096]{0:T(1024)} %bitcast.78, f32[16]{0:T(128)S(1)} %add_rsqrt_fusion.3), kind=kOutput, calls=%fused_computation.11.clone.1 | convolution fusion | flops 402915328 | bytes 25509952 | tf_op jit(solution)/shard_map/while/body/eval_jaxpr/bd,jdc->jbc/dot_general | solution.py:81
  148.7 5.3 %fusion.43 = f32[16,4096]{1,0:T(8,128)} fusion(bf16[1024,4096]{1,0:T(8,128)(2,1)} %get-tuple-element.560, f32[16,1024]{1,0:T(8,128)S(1)} %get-tuple-element.481, f32[3,16,1024]{2,1,0:T(8,128)S(1)} %convolution_bitcast_fusion.2), kind=kOutput, calls=%fused_computation.28.clone.1 | convolution fusion | flops 134250496 | bytes 8781824 | tf_op jit(solution)/shard_map/while/body/eval_jaxpr/dot_general | solution.py:98
  157.8 15.5 %reduce-scatter.6.cloned.1.call-done = f32[16,1024]{1,0:T(8,128)} async-done(((f32[16,4096]{1,0:T(8,128)}), f32[16,1024]{1,0:T(8,128)}) %reduce-scatter.6.cloned.1.call-update) | async-done | bytes 65552 | tf_op jit(solution)/shard_map/while/body/eval_jaxpr/reduce_scatter | solution.py:99
  174.3 3.4 collective-permute-start
  182.6 2.0 gather_fusion
  184.7 5.4 %all_gather.12 = bf16[16,4096]{1,0:T(8,128)(2,1)S(1)} all-gather(bf16[16,1024]{1,0:T(8,128)(2,1)S(1)} %select_select_fusion.2), channel_id=1, replica_groups=mesh['groups'=2,'segment'=4,'inner'=4] {'inner'}, dimensions={1}, use_global_device_ids=true | all-gather | bytes 163840 | tf_op jit(solution)/shard_map/while/body/eval_jaxpr/all_gather | solution.py:79
  190.3 10.0 %convolution_bitcast_fusion.2 = f32[3,16,1024]{2,1,0:T(8,128)S(1)} fusion(bf16[3,4096,1024]{2,1,0:T(8,128)(2,1)} %get-tuple-element.555, bf16[16,4096]{1,0:T(8,128)(2,1)S(1)} %all_gather.12, f32[4096]{0:T(1024)} %bitcast.78, f32[16]{0:T(128)S(1)} %add_rsqrt_fusion.3), kind=kOutput, calls=%fused_computation.11.clone.1 | convolution fusion | flops 402915328 | bytes 25509952 | tf_op jit(solution)/shard_map/while/body/eval_jaxpr/bd,jdc->jbc/dot_general | solution.py:81
  201.0 5.3 %fusion.43 = f32[16,4096]{1,0:T(8,128)} fusion(bf16[1024,4096]{1,0:T(8,128)(2,1)} %get-tuple-element.560, f32[16,1024]{1,0:T(8,128)S(1)} %get-tuple-element.481, f32[3,16,1024]{2,1,0:T(8,128)S(1)} %convolution_bitcast_fusion.2), kind=kOutput, calls=%fused_computation.28.clone.1 | convolution fusion | flops 134250496 | bytes 8781824 | tf_op jit(solution)/shard_map/while/body/eval_jaxpr/dot_general | solution.py:98
  210.2 15.5 %reduce-scatter.6.cloned.1.call-done = f32[16,1024]{1,0:T(8,128)} async-done(((f32[16,4096]{1,0:T(8,128)}), f32[16,1024]{1,0:T(8,128)}) %reduce-scatter.6.cloned.1.call-update) | async-done | bytes 65552 | tf_op jit(solution)/shard_map/while/body/eval_jaxpr/reduce_scatter | solution.py:99
  226.6 3.4 collective-permute-start
  235.0 2.0 gather_fusion
  237.0 5.4 %all_gather.12 = bf16[16,4096]{1,0:T(8,128)(2,1)S(1)} all-gather(bf16[16,1024]{1,0:T(8,128)(2,1)S(1)} %select_select_fusion.2), channel_id=1, replica_groups=mesh['groups'=2,'segment'=4,'inner'=4] {'inner'}, dimensions={1}, use_global_device_ids=true | all-gather | bytes 163840 | tf_op jit(solution)/shard_map/while/body/eval_jaxpr/all_gather | solution.py:79
  242.6 10.0 %convolution_bitcast_fusion.2 = f32[3,16,1024]{2,1,0:T(8,128)S(1)} fusion(bf16[3,4096,1024]{2,1,0:T(8,128)(2,1)} %get-tuple-element.555, bf16[16,4096]{1,0:T(8,128)(2,1)S(1)} %all_gather.12, f32[4096]{0:T(1024)} %bitcast.78, f32[16]{0:T(128)S(1)} %add_rsqrt_fusion.3), kind=kOutput, calls=%fused_computation.11.clone.1 | convolution fusion | flops 402915328 | bytes 25509952 | tf_op jit(solution)/shard_map/while/body/eval_jaxpr/bd,jdc->jbc/dot_general | solution.py:81
  253.3 5.3 %fusion.43 = f32[16,4096]{1,0:T(8,128)} fusion(bf16[1024,4096]{1,0:T(8,128)(2,1)} %get-tuple-element.560, f32[16,1024]{1,0:T(8,128)S(1)} %get-tuple-element.481, f32[3,16,1024]{2,1,0:T(8,128)S(1)} %convolution_bitcast_fusion.2), kind=kOutput, calls=%fused_computation.28.clone.1 | convolution fusion | flops 134250496 | bytes 8781824 | tf_op jit(solution)/shard_map/while/body/eval_jaxpr/dot_general | solution.py:98
  262.5 15.5 %reduce-scatter.6.cloned.1.call-done = f32[16,1024]{1,0:T(8,128)} async-done(((f32[16,4096]{1,0:T(8,128)}), f32[16,1024]{1,0:T(8,128)}) %reduce-scatter.6.cloned.1.call-update) | async-done | bytes 65552 | tf_op jit(solution)/shard_map/while/body/eval_jaxpr/reduce_scatter | solution.py:99
  278.9 3.4 collective-permute-start
  287.3 2.0 gather_fusion
  289.4 5.4 %all_gather.12 = bf16[16,4096]{1,0:T(8,128)(2,1)S(1)} all-gather(bf16[16,1024]{1,0:T(8,128)(2,1)S(1)} %select_select_fusion.2), channel_id=1, replica_groups=mesh['groups'=2,'segment'=4,'inner'=4] {'inner'}, dimensions={1}, use_global_device_ids=true | all-gather | bytes 163840 | tf_op jit(solution)/shard_map/while/body/eval_jaxpr/all_gather | solution.py:79
  294.9 10.0 %convolution_bitcast_fusion.2 = f32[3,16,1024]{2,1,0:T(8,128)S(1)} fusion(bf16[3,4096,1024]{2,1,0:T(8,128)(2,1)} %get-tuple-element.555, bf16[16,4096]{1,0:T(8,128)(2,1)S(1)} %all_gather.12, f32[4096]{0:T(1024)} %bitcast.78, f32[16]{0:T(128)S(1)} %add_rsqrt_fusion.3), kind=kOutput, calls=%fused_computation.11.clone.1 | convolution fusion | flops 402915328 | bytes 25509952 | tf_op jit(solution)/shard_map/while/body/eval_jaxpr/bd,jdc->jbc/dot_general | solution.py:81
  305.7 5.3 %fusion.43 = f32[16,4096]{1,0:T(8,128)} fusion(bf16[1024,4096]{1,0:T(8,128)(2,1)} %get-tuple-element.560, f32[16,1024]{1,0:T(8,128)S(1)} %get-tuple-element.481, f32[3,16,1024]{2,1,0:T(8,128)S(1)} %convolution_bitcast_fusion.2), kind=kOutput, calls=%fused_computation.28.clone.1 | convolution fusion | flops 134250496 | bytes 8781824 | tf_op jit(solution)/shard_map/while/body/eval_jaxpr/dot_general | solution.py:98
  314.8 15.5 %reduce-scatter.6.cloned.1.call-done = f32[16,1024]{1,0:T(8,128)} async-done(((f32[16,4096]{1,0:T(8,128)}), f32[16,1024]{1,0:T(8,128)}) %reduce-scatter.6.cloned.1.call-update) | async-done | bytes 65552 | tf_op jit(solution)/shard_map/while/body/eval_jaxpr/reduce_scatter | solution.py:99
  331.2 3.4 collective-permute-start
  341.7 5.4 %all_gather.12 = bf16[16,4096]{1,0:T(8,128)(2,1)S(1)} all-gather(bf16[16,1024]{1,0:T(8,128)(2,1)S(1)} %select_select_fusion.2), channel_id=1, replica_groups=mesh['groups'=2,'segment'=4,'inner'=4] {'inner'}, dimensions={1}, use_global_device_ids=true | all-gather | bytes 163840 | tf_op jit(solution)/shard_map/while/body/eval_jaxpr/all_gather | solution.py:79
  347.2 10.0 %convolution_bitcast_fusion.2 = f32[3,16,1024]{2,1,0:T(8,128)S(1)} fusion(bf16[3,4096,1024]{2,1,0:T(8,128)(2,1)} %get-tuple-element.555, bf16[16,4096]{1,0:T(8,128)(2,1)S(1)} %all_gather.12, f32[4096]{0:T(1024)} %bitcast.78, f32[16]{0:T(128)S(1)} %add_rsqrt_fusion.3), kind=kOutput, calls=%fused_computation.11.clone.1 | convolution fusion | flops 402915328 | bytes 25509952 | tf_op jit(solution)/shard_map/while/body/eval_jaxpr/bd,jdc->jbc/dot_general | solution.py:81
  358.0 5.3 %fusion.43 = f32[16,4096]{1,0:T(8,128)} fusion(bf16[1024,4096]{1,0:T(8,128)(2,1)} %get-tuple-element.560, f32[16,1024]{1,0:T(8,128)S(1)} %get-tuple-element.481, f32[3,16,1024]{2,1,0:T(8,128)S(1)} %convolution_bitcast_fusion.2), kind=kOutput, calls=%fused_computation.28.clone.1 | convolution fusion | flops 134250496 | bytes 8781824 | tf_op jit(solution)/shard_map/while/body/eval_jaxpr/dot_general | solution.py:98
  367.1 15.5 %reduce-scatter.6.cloned.1.call-done = f32[16,1024]{1,0:T(8,128)} async-done(((f32[16,4096]{1,0:T(8,128)}), f32[16,1024]{1,0:T(8,128)}) %reduce-scatter.6.cloned.1.call-update) | async-done | bytes 65552 | tf_op jit(solution)/shard_map/while/body/eval_jaxpr/reduce_scatter | solution.py:99
  383.5 6.5 %all_gather.9 = bf16[2,32,4096]{2,1,0:T(8,128)(2,1)S(1)} all-gather(bf16[2,32,1024]{2,1,0:T(8,128)(2,1)S(1)} %get-tuple-element.257), channel_id=1, replica_groups=mesh['groups'=2,'segment'=4,'inner'=4] {'inner'}, dimensions={2}, use_global_device_ids=true | all-gather | bytes 655360 | tf_op jit(solution)/shard_map/all_gather | solution.py:119
  391.3 2.6 copy.27
  393.8 6.7 %all-reduce.1 = (f32[2,32]{1,0:T(2,128)S(1)}, f32[2,32]{1,0:T(2,128)S(1)}) all-reduce(f32[2,32]{1,0:T(2,128)S(1)} %get-tuple-element.321, f32[2,32]{1,0:T(2,128)S(1)} %get-tuple-element.320), channel_id=1, replica_groups=mesh['groups'=2,'segment'=4,'inner'=4] {'inner'}, use_global_device_ids=true, to_apply=%region_11.12 | all-reduce | flops 128 | bytes 1024 | tf_op jit(solution)/shard_map/psum | solution.py:129
  400.6 11.7 %all-reduce = f32[2,32]{1,0:T(2,128)S(1)} all-reduce(f32[2,32]{1,0:T(2,128)S(1)} %subtract_select_fusion), channel_id=4, replica_groups=mesh['groups'=2,'segment'=4,'inner'=4] {'segment'}, use_global_device_ids=true, to_apply=%region_14.15.clone | all-reduce | flops 64 | bytes 512
  (211 shorter events, 80.9 us)
Async XLA Ops:
  8.0 382.3 %copy-start = (bf16[4096,128]{1,0:T(8,128)(2,1)S(1)}, bf16[4096,128]{1,0:T(8,128)(2,1)}, u32[]{:S(2)}) copy-start(bf16[4096,128]{1,0:T(8,128)(2,1)} %param.27) | copy-start | bytes 3145732
  14.5 375.8 %copy-start.3 = (f32[4096]{0:T(1024)S(1)}, f32[4096]{0:T(1024)}, u32[]{:S(2)}) copy-start(f32[4096]{0:T(1024)} %param.26) | copy-start | bytes 49156
  14.5 397.8 %copy-start.4 = (u32[32]{0:T(128)S(1)}, u32[32]{0:T(128)}, u32[]{:S(2)}) copy-start(u32[32]{0:T(128)} %constant.157) | copy-start | bytes 388
  14.5 54.2 %reduce-scatter.6.cloned.1.call-start = ((), (), s32[]{:S(2)}) async-start(), calls=%async_computation.3 | async-start | bytes 327680 | tf_op jit(solution)/shard_map/while/body/eval_jaxpr/reduce_scatter | solution.py:99
  14.6 11.9 %collective-permute-start = (bf16[16,1024]{1,0:T(8,128)(2,1)S(1)}, bf16[16,1024]{1,0:T(8,128)(2,1)S(1)}, u32[]{:S(2)}, u32[]{:S(2)}) collective-permute-start(bf16[16,1024]{1,0:T(8,128)(2,1)S(1)} %broadcast_select_fusion.3), channel_id=1, source_target_pairs={{0,4},{4,8},{8,12},{1,5},{5,9},{9,13},{2,6},{6,10},{10,14},{3,7},{... | collective-permute-start | bytes 98312 | tf_op jit(solution)/shard_map/while/body/eval_jaxpr/ppermute | solution.py:12
  26.5 15.7 %copy-start.1 = (f32[1,8,1024]{2,1,0:T(8,128)S(1)}, f32[1,8,1024]{2,1,0:T(8,128)}, u32[]{:S(2)}) copy-start(f32[1,8,1024]{2,1,0:T(8,128)} %get-tuple-element.557) | copy-start | bytes 98308 | tf_op jit(solution)/shard_map/while
  26.5 15.6 %copy-start.2 = (f32[8,1024]{1,0:T(8,128)S(1)}, f32[8,1024]{1,0:T(8,128)}, u32[]{:S(2)}) copy-start(f32[8,1024]{1,0:T(8,128)} %get-tuple-element.558) | copy-start | bytes 98308 | tf_op jit(solution)/shard_map/while
  69.5 51.5 %reduce-scatter.6.cloned.1.call-start = ((), (), s32[]{:S(2)}) async-start(), calls=%async_computation.3 | async-start | bytes 327680 | tf_op jit(solution)/shard_map/while/body/eval_jaxpr/reduce_scatter | solution.py:99
  69.6 10.4 %collective-permute-start = (bf16[16,1024]{1,0:T(8,128)(2,1)S(1)}, bf16[16,1024]{1,0:T(8,128)(2,1)S(1)}, u32[]{:S(2)}, u32[]{:S(2)}) collective-permute-start(bf16[16,1024]{1,0:T(8,128)(2,1)S(1)} %broadcast_select_fusion.3), channel_id=1, source_target_pairs={{0,4},{4,8},{8,12},{1,5},{5,9},{9,13},{2,6},{6,10},{10,14},{3,7},{... | collective-permute-start | bytes 98312 | tf_op jit(solution)/shard_map/while/body/eval_jaxpr/ppermute | solution.py:12
  80.0 15.7 %copy-start.1 = (f32[1,8,1024]{2,1,0:T(8,128)S(1)}, f32[1,8,1024]{2,1,0:T(8,128)}, u32[]{:S(2)}) copy-start(f32[1,8,1024]{2,1,0:T(8,128)} %get-tuple-element.557) | copy-start | bytes 98308 | tf_op jit(solution)/shard_map/while
  80.0 15.6 %copy-start.2 = (f32[8,1024]{1,0:T(8,128)S(1)}, f32[8,1024]{1,0:T(8,128)}, u32[]{:S(2)}) copy-start(f32[8,1024]{1,0:T(8,128)} %get-tuple-element.558) | copy-start | bytes 98308 | tf_op jit(solution)/shard_map/while
  121.9 51.5 %reduce-scatter.6.cloned.1.call-start = ((), (), s32[]{:S(2)}) async-start(), calls=%async_computation.3 | async-start | bytes 327680 | tf_op jit(solution)/shard_map/while/body/eval_jaxpr/reduce_scatter | solution.py:99
  121.9 10.4 %collective-permute-start = (bf16[16,1024]{1,0:T(8,128)(2,1)S(1)}, bf16[16,1024]{1,0:T(8,128)(2,1)S(1)}, u32[]{:S(2)}, u32[]{:S(2)}) collective-permute-start(bf16[16,1024]{1,0:T(8,128)(2,1)S(1)} %broadcast_select_fusion.3), channel_id=1, source_target_pairs={{0,4},{4,8},{8,12},{1,5},{5,9},{9,13},{2,6},{6,10},{10,14},{3,7},{... | collective-permute-start | bytes 98312 | tf_op jit(solution)/shard_map/while/body/eval_jaxpr/ppermute | solution.py:12
  132.3 15.7 %copy-start.1 = (f32[1,8,1024]{2,1,0:T(8,128)S(1)}, f32[1,8,1024]{2,1,0:T(8,128)}, u32[]{:S(2)}) copy-start(f32[1,8,1024]{2,1,0:T(8,128)} %get-tuple-element.557) | copy-start | bytes 98308 | tf_op jit(solution)/shard_map/while
  132.3 15.6 %copy-start.2 = (f32[8,1024]{1,0:T(8,128)S(1)}, f32[8,1024]{1,0:T(8,128)}, u32[]{:S(2)}) copy-start(f32[8,1024]{1,0:T(8,128)} %get-tuple-element.558) | copy-start | bytes 98308 | tf_op jit(solution)/shard_map/while
  174.2 51.4 %reduce-scatter.6.cloned.1.call-start = ((), (), s32[]{:S(2)}) async-start(), calls=%async_computation.3 | async-start | bytes 327680 | tf_op jit(solution)/shard_map/while/body/eval_jaxpr/reduce_scatter | solution.py:99
  174.3 10.4 %collective-permute-start = (bf16[16,1024]{1,0:T(8,128)(2,1)S(1)}, bf16[16,1024]{1,0:T(8,128)(2,1)S(1)}, u32[]{:S(2)}, u32[]{:S(2)}) collective-permute-start(bf16[16,1024]{1,0:T(8,128)(2,1)S(1)} %broadcast_select_fusion.3), channel_id=1, source_target_pairs={{0,4},{4,8},{8,12},{1,5},{5,9},{9,13},{2,6},{6,10},{10,14},{3,7},{... | collective-permute-start | bytes 98312 | tf_op jit(solution)/shard_map/while/body/eval_jaxpr/ppermute | solution.py:12
  184.6 15.7 %copy-start.1 = (f32[1,8,1024]{2,1,0:T(8,128)S(1)}, f32[1,8,1024]{2,1,0:T(8,128)}, u32[]{:S(2)}) copy-start(f32[1,8,1024]{2,1,0:T(8,128)} %get-tuple-element.557) | copy-start | bytes 98308 | tf_op jit(solution)/shard_map/while
  184.6 15.6 %copy-start.2 = (f32[8,1024]{1,0:T(8,128)S(1)}, f32[8,1024]{1,0:T(8,128)}, u32[]{:S(2)}) copy-start(f32[8,1024]{1,0:T(8,128)} %get-tuple-element.558) | copy-start | bytes 98308 | tf_op jit(solution)/shard_map/while
  226.5 51.4 %reduce-scatter.6.cloned.1.call-start = ((), (), s32[]{:S(2)}) async-start(), calls=%async_computation.3 | async-start | bytes 327680 | tf_op jit(solution)/shard_map/while/body/eval_jaxpr/reduce_scatter | solution.py:99
  226.6 10.4 %collective-permute-start = (bf16[16,1024]{1,0:T(8,128)(2,1)S(1)}, bf16[16,1024]{1,0:T(8,128)(2,1)S(1)}, u32[]{:S(2)}, u32[]{:S(2)}) collective-permute-start(bf16[16,1024]{1,0:T(8,128)(2,1)S(1)} %broadcast_select_fusion.3), channel_id=1, source_target_pairs={{0,4},{4,8},{8,12},{1,5},{5,9},{9,13},{2,6},{6,10},{10,14},{3,7},{... | collective-permute-start | bytes 98312 | tf_op jit(solution)/shard_map/while/body/eval_jaxpr/ppermute | solution.py:12
  236.9 15.7 %copy-start.1 = (f32[1,8,1024]{2,1,0:T(8,128)S(1)}, f32[1,8,1024]{2,1,0:T(8,128)}, u32[]{:S(2)}) copy-start(f32[1,8,1024]{2,1,0:T(8,128)} %get-tuple-element.557) | copy-start | bytes 98308 | tf_op jit(solution)/shard_map/while
  236.9 15.6 %copy-start.2 = (f32[8,1024]{1,0:T(8,128)S(1)}, f32[8,1024]{1,0:T(8,128)}, u32[]{:S(2)}) copy-start(f32[8,1024]{1,0:T(8,128)} %get-tuple-element.558) | copy-start | bytes 98308 | tf_op jit(solution)/shard_map/while
  278.8 51.4 %reduce-scatter.6.cloned.1.call-start = ((), (), s32[]{:S(2)}) async-start(), calls=%async_computation.3 | async-start | bytes 327680 | tf_op jit(solution)/shard_map/while/body/eval_jaxpr/reduce_scatter | solution.py:99
  278.9 10.4 %collective-permute-start = (bf16[16,1024]{1,0:T(8,128)(2,1)S(1)}, bf16[16,1024]{1,0:T(8,128)(2,1)S(1)}, u32[]{:S(2)}, u32[]{:S(2)}) collective-permute-start(bf16[16,1024]{1,0:T(8,128)(2,1)S(1)} %broadcast_select_fusion.3), channel_id=1, source_target_pairs={{0,4},{4,8},{8,12},{1,5},{5,9},{9,13},{2,6},{6,10},{10,14},{3,7},{... | collective-permute-start | bytes 98312 | tf_op jit(solution)/shard_map/while/body/eval_jaxpr/ppermute | solution.py:12
  289.2 15.7 %copy-start.1 = (f32[1,8,1024]{2,1,0:T(8,128)S(1)}, f32[1,8,1024]{2,1,0:T(8,128)}, u32[]{:S(2)}) copy-start(f32[1,8,1024]{2,1,0:T(8,128)} %get-tuple-element.557) | copy-start | bytes 98308 | tf_op jit(solution)/shard_map/while
  289.3 15.6 %copy-start.2 = (f32[8,1024]{1,0:T(8,128)S(1)}, f32[8,1024]{1,0:T(8,128)}, u32[]{:S(2)}) copy-start(f32[8,1024]{1,0:T(8,128)} %get-tuple-element.558) | copy-start | bytes 98308 | tf_op jit(solution)/shard_map/while
  331.2 51.4 %reduce-scatter.6.cloned.1.call-start = ((), (), s32[]{:S(2)}) async-start(), calls=%async_computation.3 | async-start | bytes 327680 | tf_op jit(solution)/shard_map/while/body/eval_jaxpr/reduce_scatter | solution.py:99
  331.2 10.4 %collective-permute-start = (bf16[16,1024]{1,0:T(8,128)(2,1)S(1)}, bf16[16,1024]{1,0:T(8,128)(2,1)S(1)}, u32[]{:S(2)}, u32[]{:S(2)}) collective-permute-start(bf16[16,1024]{1,0:T(8,128)(2,1)S(1)} %broadcast_select_fusion.3), channel_id=1, source_target_pairs={{0,4},{4,8},{8,12},{1,5},{5,9},{9,13},{2,6},{6,10},{10,14},{3,7},{... | collective-permute-start | bytes 98312 | tf_op jit(solution)/shard_map/while/body/eval_jaxpr/ppermute | solution.py:12
  341.6 15.7 %copy-start.1 = (f32[1,8,1024]{2,1,0:T(8,128)S(1)}, f32[1,8,1024]{2,1,0:T(8,128)}, u32[]{:S(2)}) copy-start(f32[1,8,1024]{2,1,0:T(8,128)} %get-tuple-element.557) | copy-start | bytes 98308 | tf_op jit(solution)/shard_map/while
  341.6 15.6 %copy-start.2 = (f32[8,1024]{1,0:T(8,128)S(1)}, f32[8,1024]{1,0:T(8,128)}, u32[]{:S(2)}) copy-start(f32[8,1024]{1,0:T(8,128)} %get-tuple-element.558) | copy-start | bytes 98308 | tf_op jit(solution)/shard_map/while
  383.5 30.7 %reduce-scatter.4.cloned.1.call-start = ((), (), s32[]{:S(2)}) async-start(), calls=%async_computation.2 | async-start | bytes 40960 | tf_op jit(solution)/shard_map/reduce_scatter | solution.py:134
Sparse Core Ops, SparseCore 0:
  48.3 20.2 reduce-scatter.5
  101.8 19.1 reduce-scatter.5
  154.1 19.1 reduce-scatter.5
  206.5 19.1 reduce-scatter.5
  258.8 19.1 reduce-scatter.5
  311.1 19.1 reduce-scatter.5
  363.4 19.1 reduce-scatter.5
Sparse Core Ops, SparseCore 1:
  391.4 19.8 reduce-scatter.3
where the time goes:
time: 425 us; the launch traced here: 422 us
  waiting for transfers between devices  110 us (26%)
  matrix products  108 us (25%)
  blocking collectives  62.8 us (15%)
  other arithmetic  48.1 us (11%)
  local copies, waits for them, and re-layouts  45.5 us (11%)
  starting transfers between devices  25.7 us (6%)
  between operations  16.2 us (4%)
  loops' own time  6.16 us (1%)
    reduce_scatter x7, waiting for transfers between devices, advance(): lax.psum_scatter(partial_sum, 'inner', scatter_dimension=1, tiled=True)  109 us
    dot_general x7, matrix products, advance(): jnp.einsum('bd,jdc->jbc', normalized, w_in, preferred_element_type=jnp.fl...  69.7 us
    all_gather x7, blocking collectives, advance(): gathered = lax.all_gather(stream_in, 'inner', axis=1, tiled=True)  37.8 us
    dot_general x7, matrix products, advance(): partial_sum = jnp.dot(gated_rows, w_out, preferred_element_type=jnp.float32)  37.1 us
    ppermute x7, starting transfers between devices, from_behind(): return lax.ppermute(block, axis, route)  25.3 us
    gather x7, local copies, waits for them, and re-layouts, advance(): looked_up = jnp.take(embedding, token_ids, axis=0)  13.8 us
    dynamic_update_slice x7, other arithmetic, advance(): lax.dynamic_update_slice_in_dim(fir_all, jnp.where(is_valid, fir_next, fi...  13.4 us
    dynamic_update_slice x7, other arithmetic, advance(): lax.dynamic_update_slice_in_dim(modal_all, jnp.where(is_valid, modal_next...  13.2 us
  transfers between devices with their start and end apart: 15, of which 7 were waited for; matrix products, arithmetic and copies ran while one was open for 18% of the time, Pallas kernels for 0%

commit v1 on v0

v1 whole, which is shorter than its diff:
```python
import functools

import jax
import jax.numpy as jnp
from jax import lax
from jax.experimental import pallas as pl
from jax.experimental.pallas import tpu as pltpu
from jax.sharding import PartitionSpec as P

EPS = 1e-05
BOTH = ("segment", "inner")
VM = pl.BlockSpec(memory_space=pltpu.VMEM)


def in_kernel_memory(array):
    return pltpu.with_memory_space_constraint(array, pltpu.VMEM)


def lanes(index, width):
    return pl.ds(pl.multiple_of(index * width, width), width)


def column_tile(width):
    return min(512, width)


def dot(left, right):
    return jnp.dot(left, right, preferred_element_type=jnp.float32)


def scaled_half(half_ref, gain_ref, scaled, core, chips, width):
    total = None
    for chip in range(chips):
        values = half_ref[:, chip * width : (chip + 1) * width].astype(jnp.float32)
        part = jnp.sum(values * values, axis=-1, keepdims=True)
        total = part if total is None else total + part
        gain = gain_ref[:, lanes(2 * chip + core, width)]
        scaled[:, chip * width : (chip + 1) * width] = (values * gain).astype(jnp.bfloat16)
    return total


def half_product(scaled, w_in, part, core, columns, chips, width):
    total = None
    for chip in range(chips):
        rows = lanes(2 * chip + core, width)
        term = dot(scaled[:, chip * width : (chip + 1) * width], w_in[part, rows, columns])
        total = term if total is None else total + term
    return total


def first_kernel(stage, chips, own, gain, w_in, sums, squares, scaled):
    width = w_in.shape[2]
    tile = column_tile(width)

    @pl.when(lax.axis_index("segment") == stage)
    def _():
        core = lax.rem(lax.axis_index("inner"), 2)
        total = scaled_half(own, gain, scaled, core, chips, width)
        squares[...] = jnp.broadcast_to(total, squares.shape)
        for part in range(3):

            @pl.loop(0, width // tile)
            def _(step):
                columns = lanes(step, tile)
                sums[part, :, columns] = half_product(
                    scaled, w_in, part, core, columns, chips, width
                )


def second_kernel(
    stage,
    chips,
    steps,
    other,
    gain,
    w_in,
    sums,
    squares,
    fixed,
    factors,
    product_in,
    w_out,
    product,
    gated,
    partner,
    scaled,
):
    width = w_in.shape[2]
    tile = column_tile(width)
    seqs = other.shape[0] // steps
    features = w_in.shape[1]

    @pl.when(lax.axis_index("segment") == stage)
    def _():
        core = lax.rem(lax.axis_index("inner"), 2)
        facing = 1 - core
        total = scaled_half(other, gain, scaled, facing, chips, width)
        mean_square = (total + squares[:, :1]) / features
        scale = lax.rsqrt(mean_square + EPS)

        @pl.loop(0, width // tile)
        def _(step):
            columns = lanes(step, tile)
            query, key, value = (
                scale
                * (
                    sums[part, :, columns]
                    + half_product(scaled, w_in, part, facing, columns, chips, width)
                )
                for part in range(3)
            )
            fresh = key * value
            product[:, columns] = fresh
            for now in range(steps):
                rows = slice(now * seqs, (now + 1) * seqs)
                filtered = fixed[now, :, columns]
                for back in range(now + 1):
                    source = slice((now - back) * seqs, (now - back + 1) * seqs)
                    filtered = filtered + factors[back : back + 1, columns] * fresh[source]
                gated[rows, columns] = (query[rows] * filtered).astype(jnp.bfloat16)

        out_half(gated, w_out, partner, facing, chips)


def out_half(gated, w_out, result, core, chips):
    width = w_out.shape[1] // (2 * chips)
    tile = column_tile(width)
    for chip in range(chips):

        @pl.loop(0, width // tile)
        def _(step):
            source = pl.ds(pl.multiple_of((2 * chip + core) * width + step * tile, tile), tile)
            target = pl.ds(pl.multiple_of(chip * width + step * tile, tile), tile)
            result[:, target] = dot(gated[...], w_out[:, source]).astype(result.dtype)


def third_kernel(stage, chips, gated, w_out, result):
    @pl.when(lax.axis_index("segment") == stage)
    def _():
        core = lax.rem(lax.axis_index("inner"), 2)
        out_half(gated, w_out, result, core, chips)


def call(kernel, outs, args, scratch=(), aliases=None, flops=0, nbytes=0):
    return pl.pallas_call(
        kernel,
        out_shape=outs,
        in_specs=[VM] * len(args),
        out_specs=jax.tree.map(lambda _: VM, outs),
        scratch_shapes=scratch,
        input_output_aliases=aliases or {},
        compiler_params=pltpu.CompilerParams(vmem_limit_bytes=8 << 20),
        cost_estimate=pl.CostEstimate(flops=flops, bytes_accessed=nbytes, transcendentals=0),
    )(*args)


def head_kernel(
    chips, own, other, gain, unembed, targets, columns, logits, sums, head_in
):
    width = gain.shape[1] // (2 * chips)
    core = lax.rem(lax.axis_index("inner"), 2)
    total = jnp.zeros((own.shape[0], 1), jnp.float32)
    for half_ref in (own, other):
        values = half_ref[...].astype(jnp.float32)
        total = total + jnp.sum(values * values, axis=-1, keepdims=True)
    scale = lax.rsqrt(total / gain.shape[1] + EPS)
    for half_ref, which in ((own, core), (other, 1 - core)):
        for chip in range(chips):
            values = half_ref[:, chip * width : (chip + 1) * width].astype(jnp.float32)
            place = lanes(2 * chip + which, width)
            head_in[:, place] = (values * scale * gain[:, place]).astype(jnp.bfloat16)
    result = dot(head_in[...], unembed[...])
    logits[...] = result
    exp_local = jnp.sum(jnp.exp(result), axis=-1, keepdims=True)
    here = columns[...] == targets[...]
    target_local = jnp.sum(jnp.where(here, result, 0.0), axis=-1, keepdims=True)
    place = lax.broadcasted_iota(jnp.int32, sums.shape, 1)
    sums[...] = jnp.where(place == 0, exp_local, target_local)


def swap_cores(block):
    count = lax.axis_size("inner")
    return lax.ppermute(block, "inner", [(i, i ^ 1) for i in range(count)])


def short_parts(fir, taps, steps):
    held = fir.shape[1]
    fixed = []
    for now in range(steps):
        total = jnp.zeros(fir.shape[:1] + fir.shape[2:], jnp.float32)
        for back in range(now + 1, held + 1):
            total = total + fir[:, held - (back - now)] * taps[back]
        fixed.append(total)
    return jnp.stack(fixed), taps[:steps]


def modal_parts(modal, taps, rate, residue, steps):
    decay = jnp.exp(-rate)
    fixed, factors = [], []
    power = jnp.ones_like(decay)
    for now in range(steps):
        factor = jnp.sum(residue * power * (1.0 - decay), axis=0)
        factors.append(factor + taps[0] if now == 0 else factor)
        power = power * decay
        fixed.append(jnp.sum((residue * power)[None] * modal, axis=1))
    return jnp.stack(fixed), jnp.stack(factors)


def per_device(
    tokens,
    embedding,
    in_proj,
    out_proj,
    norm_gain,
    fir_taps,
    modal_rate,
    modal_residue,
    fir_state,
    modal_state,
    final_gain,
    unembed,
):
    segments = lax.axis_size("segment")
    count = lax.axis_size("inner")
    chips = count // 2
    segment = lax.axis_index("segment")
    inner = lax.axis_index("inner")
    steps = tokens.shape[0] - 1
    seqs = tokens.shape[1]
    rows = steps * seqs
    width = embedding.shape[1]
    half = chips * width
    features = half * 2
    w_in = in_kernel_memory(in_proj[0])
    w_out = in_kernel_memory(out_proj[0])
    is_short = segment % 2 == 0
    taps, rate, residue = fir_taps[0], modal_rate[0], modal_residue[0]
    fir, modal = fir_state[0], modal_state[0]

    short_fixed, short_factors = short_parts(fir, taps, steps)
    modal_fixed, modal_factors = modal_parts(modal, taps, rate, residue, steps)
    fixed = jnp.where(is_short, short_fixed, modal_fixed)
    factors = jnp.where(is_short, short_factors, modal_factors)

    picked = jnp.take(embedding, tokens[:steps].reshape(rows), axis=0)
    pieces = [None] * chips
    for hop in range(chips):
        route = [(i, (i + 2 * hop) % count) for i in range(count)]
        pieces[hop] = lax.ppermute(picked, "inner", route) if hop else picked
    chip_here = inner // 2
    stacked = jnp.stack(pieces)
    order = (chip_here - jnp.arange(chips)) % chips
    own = jnp.concatenate([stacked[order[c]] for c in range(chips)], axis=1)

    product = jnp.zeros((rows, width), jnp.float32)
    f32, bf16 = jnp.float32, jnp.bfloat16
    shape = jax.ShapeDtypeStruct
    for stage in range(segments):
        other = swap_cores(own)
        sums, squares = call(
            functools.partial(first_kernel, stage, chips),
            (shape((3, rows, width), f32), shape((rows, 128), f32)),
            (own, norm_gain, w_in),
            scratch=[pltpu.VMEM((rows, half), bf16)],
            flops=6 * rows * half * width,
            nbytes=6 * half * width,
        )
        product, gated, partner = call(
            functools.partial(second_kernel, stage, chips, steps),
            (shape((rows, width), f32), shape((rows, width), bf16), shape((rows, half), bf16)),
            (other, norm_gain, w_in, sums, squares, fixed, factors, product, w_out),
            scratch=[pltpu.VMEM((rows, half), bf16)],
            aliases={7: 0},
            flops=8 * rows * half * width,
            nbytes=8 * half * width,
        )
        facing = swap_cores(partner)
        mine = call(
            functools.partial(third_kernel, stage, chips),
            shape((rows, half), f32),
            (gated, w_out),
            flops=2 * rows * half * width,
            nbytes=2 * half * width,
        )
        share = own.astype(f32) * (1.0 / chips)
        chip_sum = (mine + facing.astype(f32) + share).astype(bf16)
        if stage < segments - 1:
            total = None
            for hop in range(chips):
                route = [
                    (stage * count + i, (stage + 1) * count + (i + 2 * hop) % count)
                    for i in range(count)
                ]
                term = lax.ppermute(chip_sum, BOTH, route).astype(f32)
                total = term if total is None else total + term
            own = total.astype(bf16)

    block = seqs // segments
    last = segments - 1
    by_block = chip_sum.reshape(steps, segments, block, half)
    total = None
    for hop in range(chips):
        for target in range(segments):
            part = by_block[:, target].reshape(steps * block, half)
            if hop == 0 and target == last:
                term = jnp.where(segment == last, part.astype(f32), 0.0)
            else:
                route = [
                    (last * count + i, target * count + (i + 2 * hop) % count)
                    for i in range(count)
                ]
                term = lax.ppermute(part, BOTH, route).astype(f32)
            total = term if total is None else total + term
    own = total.astype(bf16)
    other = swap_cores(own)
    vocab = unembed.shape[1]
    head_rows = steps * block
    wanted = lax.dynamic_slice(tokens, (1, segment * block), (steps, block))
    targets = jnp.broadcast_to(wanted.reshape(head_rows, 1), (head_rows, vocab))
    columns = jnp.broadcast_to(
        inner * vocab + jnp.arange(vocab, dtype=jnp.int32)[None], (head_rows, vocab)
    )
    logits, totals = call(
        functools.partial(head_kernel, chips),
        (shape((head_rows, vocab), f32), shape((head_rows, 128), f32)),
        (own, other, final_gain[None], in_kernel_memory(unembed), targets, columns),
        scratch=[pltpu.VMEM((head_rows, features), bf16)],
        flops=2 * head_rows * features * vocab,
        nbytes=2 * features * vocab,
    )
    totals = totals[:, :2]
    summed = totals
    for hop in range(1, count):
        route = [(i, i ^ hop if count & (count - 1) == 0 else (i + hop) % count) for i in range(count)]
        summed = summed + lax.ppermute(totals, "inner", route)
    logprob = summed[:, 1] - jnp.log(summed[:, 0])

    fresh = product.reshape(steps, seqs, width)
    fir_next = jnp.concatenate([fir, fresh.transpose(1, 0, 2)], axis=1)[:, steps:]
    decay = jnp.exp(-rate)[None]
    modal_next = modal
    for now in range(steps):
        modal_next = decay * modal_next + (1.0 - decay) * fresh[now][:, None]
    fir_out = jnp.where(is_short, fir_next, fir)
    modal_out = jnp.where(is_short, modal, modal_next)
    return (
        logits.reshape(steps, block, vocab),
        logprob.reshape(steps, block),
        fir_out[None],
        modal_out[None],
    )


def solution(mesh):
    return jax.shard_map(
        per_device,
        mesh=mesh,
        in_specs=(
            P(None, "groups"),
            P(None, "inner"),
            P("segment", None, None, "inner"),
            P("segment", "inner", None),
            P("segment", None),
            P("segment", None, "inner"),
            P("segment", None, "inner"),
            P("segment", None, "inner"),
            P("segment", "groups", None, "inner"),
            P("segment", "groups", None, "inner"),
            P(),
            P(None, "inner"),
        ),
        out_specs=(
            P(None, ("groups", "segment"), "inner"),
            P(None, ("groups", "segment")),
            P("segment", "groups", None, "inner"),
            P("segment", "groups", None, "inner"),
        ),
        check_vma=False,
    )
```

time: 425 us -> 168 us (0.40)
  matrix products: 108 us -> 0 us
  blocking collectives: 62.8 us -> 0 us
  waiting for transfers between devices: 110 us -> 72.7 us
  other arithmetic: 48.1 us -> 11.5 us
  between operations: 16.2 us -> 5.01 us
  Pallas kernels: 0 us -> 9.13 us
  starting transfers between devices: 25.7 us -> 18.9 us
  loops' own time: 6.16 us -> 0 us
  local copies, waits for them, and re-layouts: 45.5 us -> 50.2 us
    reduce_scatter x8 -> x0, waiting for transfers between devices: 109 us -> none  [the longest x7 109 us: advance(): lax.psum_scatter(partial_sum, 'inner', scatter_dimension=1, tiled=True)]
    dot_general x15 -> x0, matrix products: 108 us -> none  [the longest x7 69.7 us: advance(): jnp.einsum('bd,jdc->jbc', normalized, w_in, preferred_element_type=jnp.fl...]
    ppermute x7 -> x26, waiting for transfers between devices: 0.02 us -> 72.7 us  [the longest x7 56.5 us: per_device(): term = lax.ppermute(part, BOTH, route).astype(f32)]
    all_gather x8 -> x0, blocking collectives: 44.4 us -> none  [the longest x7 37.8 us: advance(): gathered = lax.all_gather(stream_in, 'inner', axis=1, tiled=True)]
    unnamed x11 -> x26, local copies, waits for them, and re-layouts: 6.99 us -> 45.6 us
    dynamic_update_slice x21 -> x0, other arithmetic: 32.7 us -> none  [the longest x7 13.4 us: advance(): lax.dynamic_update_slice_in_dim(fir_all, jnp.where(is_valid, fir_next, fi...]
    dynamic_slice x21 -> x1, local copies, waits for them, and re-layouts: 19.2 us -> 0.07 us  [per_device(): wanted = lax.dynamic_slice(tokens, (1, segment * block), (steps, block))]
    gather x7 -> x1, local copies, waits for them, and re-layouts: 13.8 us -> 0.71 us  [per_device(): picked = jnp.take(embedding, tokens[:steps].reshape(rows), axis=0)]
  transfers between devices with their start and end apart: 15 -> 26, of which waited for: 7 -> 7; matrix products, arithmetic and copies ran while one was open for 18% -> 8% of each run, Pallas kernels for 0% -> 3%
where the time goes in v1:
time: 168 us; the launch traced here: 167 us
  waiting for transfers between devices  72.7 us (43%)
  local copies, waits for them, and re-layouts  50.2 us (30%)
  starting transfers between devices  18.9 us (11%)
  other arithmetic  11.5 us (7%)
  Pallas kernels  9.13 us (5%)
  between operations  5.01 us (3%)
    ppermute x7, waiting for transfers between devices, per_device(): term = lax.ppermute(part, BOTH, route).astype(f32)  56.5 us
    unnamed x26, local copies, waits for them, and re-layouts  45.6 us
    ppermute x6, waiting for transfers between devices, per_device(): term = lax.ppermute(chip_sum, BOTH, route).astype(f32)  10.6 us
    pallas_call x13, Pallas kernels, call(): pl.pallas_call(kernel, out_shape=outs, in_specs=[VM] * len(args), out_spe...  9.13 us
    ppermute x7, starting transfers between devices, per_device(): term = lax.ppermute(part, BOTH, route).astype(f32)  5.91 us
    ppermute x6, starting transfers between devices, per_device(): term = lax.ppermute(chip_sum, BOTH, route).astype(f32)  5.32 us
  transfers between devices with their start and end apart: 26, of which 7 were waited for; matrix products, arithmetic and copies ran while one was open for 8% of the time, Pallas kernels for 3%

profile of v1, /device:TPU:0, one launch (start us, length us, event | category | flops | bytes accessed | tf_op | source)
XLA Modules:
  0.0 167.4 jit_solution(7800571192356606674)
XLA Ops:
  0.7 0.8 slice.107
  1.9 0.7 gather_fusion
  2.7 3.0 %collective-permute-start = (bf16[64,1024]{1,0:T(8,128)(2,1)S(1)}, bf16[64,1024]{1,0:T(8,128)(2,1)S(1)}, u32[]{:S(2)}, u32[]{:S(2)}) collective-permute-start(bf16[64,1024]{1,0:T(8,128)(2,1)S(1)} %broadcast_select_fusion), channel_id=1, source_target_pairs={{0,2},{1,3},{2,0},{3,1},{4,6},{5,7},{6,4},{7,5},{8,10},{9,11},{10,... | collective-permute-start | bytes 393224 | tf_op jit(solution)/shard_map/ppermute | solution.py:249
  5.8 0.8 multiply_bitcast_fusion
  6.6 0.8 fusion.10
  7.4 0.8 fusion.19
  8.2 0.7 bitcast_add_fusion
  8.9 1.9 %fusion = (f32[32,1024]{1,0:T(8,128)S(1)}, f32[32,1024]{1,0:T(8,128)S(1)}) fusion(f32[1,32,8,1024]{3,2,1,0:T(8,128)} %param.21, f32[8,1024]{1,0:T(8,128)S(1)} %get-tuple-element.63, f32[8,1024]{1,0:T(8,128)S(1)} %get-tuple-element.62), kind=kLoop, calls=%fused_computation.3 | loop fusion | flops 983040 | bytes 1376256 | tf_op jit(solution)/shard_map/reduce_sum | solution.py:205
  10.8 1.3 fusion.9
  12.1 0.6 fusion.20
  15.3 0.7 slice.122
  17.6 8.1 %copy-done.1 = bf16[1,3,4096,1024]{3,2,1,0:T(8,128)(2,1)S(1)} copy-done((bf16[1,3,4096,1024]{3,2,1,0:T(8,128)(2,1)S(1)}, bf16[1,3,4096,1024]{3,2,1,0:T(8,128)(2,1)}, u32[]{:S(2)}) %copy-start.1) | copy-done | bytes 25165848
  25.7 0.7 copy-done.9
  26.5 3.1 %shard_map.147 = (f32[3,64,1024]{2,1,0:T(8,128)S(1)}, f32[64,128]{1,0:T(8,128)S(1)}) custom-call(bf16[64,2048]{1,0:T(8,128)(2,1)S(1)} %pad_maximum_fusion.1.own, f32[1,4096]{1,0:T(1,128)S(1)} %copy-done.9, bf16[3,4096,1024]{2,1,0:T(8,128)(2,1)S(1)} %bitcast.121), custom_call_target="tpu_custom_call" | custom-call | flops 805306368 | bytes 12582912 | tf_op jit(solution)/shard_map/pallas_call | solution.py:145
  29.8 8.2 %copy-done.2 = bf16[1,3,4096,1024]{3,2,1,0:T(8,128)(2,1)S(1)} copy-done((bf16[1,3,4096,1024]{3,2,1,0:T(8,128)(2,1)S(1)}, bf16[1,3,4096,1024]{3,2,1,0:T(8,128)(2,1)}, u32[]{:S(2)}) %copy-start.2) | copy-done | bytes 25165848
  38.0 3.8 %shard_map.148 = (f32[64,1024]{1,0:T(8,128)S(1)}, bf16[64,1024]{1,0:T(8,128)(2,1)S(1)}, bf16[64,2048]{1,0:T(8,128)(2,1)S(1)}) custom-call(bf16[64,2048]{1,0:T(8,128)(2,1)S(1)} %collective-permute-done.1.other, f32[1,4096]{1,0:T(1,128)S(1)} %copy-done.10, bf16[3,4096,1024]{2,1,0:T(8,128)(2,1)S(1)} %bitcast.122, ...), custom_call_target="tpu_custom_call", output_to_operand_aliasing={{0}: (7, {})} | custom-call | flops 1073741824 | bytes 16777216 | tf_op jit(solution)/shard_map/pallas_call | solution.py:145
  41.9 0.6 collective-permute-start.2
  42.4 1.2 shard_map.149
  43.7 1.3 collective-permute-start.4
  45.1 1.3 collective-permute-start.3
  46.4 5.4 %collective-permute-done.4 = bf16[64,2048]{1,0:T(8,128)(2,1)S(1)} collective-permute-done((bf16[64,2048]{1,0:T(8,128)(2,1)S(1)}, bf16[64,2048]{1,0:T(8,128)(2,1)S(1)}, u32[]{:S(2)}, u32[]{:S(2)}) %collective-permute-start.4) | collective-permute-done | bytes 262176 | tf_op jit(solution)/shard_map/ppermute | solution.py:294
  51.7 5.2 %collective-permute-done.3 = bf16[64,2048]{1,0:T(8,128)(2,1)S(1)} collective-permute-done((bf16[64,2048]{1,0:T(8,128)(2,1)S(1)}, bf16[64,2048]{1,0:T(8,128)(2,1)S(1)}, u32[]{:S(2)}, u32[]{:S(2)}) %collective-permute-start.3) | collective-permute-done | bytes 262176 | tf_op jit(solution)/shard_map/ppermute | solution.py:294
  57.1 8.1 %copy-done.3 = bf16[1,3,4096,1024]{3,2,1,0:T(8,128)(2,1)S(1)} copy-done((bf16[1,3,4096,1024]{3,2,1,0:T(8,128)(2,1)S(1)}, bf16[1,3,4096,1024]{3,2,1,0:T(8,128)(2,1)}, u32[]{:S(2)}) %copy-start.3) | copy-done | bytes 25165848
  65.8 1.2 collective-permute-done.6
  67.0 0.7 collective-permute-start.8
  67.7 0.7 collective-permute-start.7
  68.9 8.2 %copy-done.4 = bf16[1,3,4096,1024]{3,2,1,0:T(8,128)(2,1)S(1)} copy-done((bf16[1,3,4096,1024]{3,2,1,0:T(8,128)(2,1)S(1)}, bf16[1,3,4096,1024]{3,2,1,0:T(8,128)(2,1)}, u32[]{:S(2)}) %copy-start.4) | copy-done | bytes 25165848
  77.2 1.4 collective-permute-done.10
  78.8 0.7 collective-permute-start.12
  79.4 0.7 collective-permute-start.11
  80.4 8.2 %copy-done.5 = bf16[1,3,4096,1024]{3,2,1,0:T(8,128)(2,1)S(1)} copy-done((bf16[1,3,4096,1024]{3,2,1,0:T(8,128)(2,1)S(1)}, bf16[1,3,4096,1024]{3,2,1,0:T(8,128)(2,1)}, u32[]{:S(2)}) %copy-start.5) | copy-done | bytes 25165848
  89.4 3.4 %copy-done.7 = bf16[1,1024,4096]{2,1,0:T(8,128)(2,1)S(1)} copy-done((bf16[1,1024,4096]{2,1,0:T(8,128)(2,1)S(1)}, bf16[1,1024,4096]{2,1,0:T(8,128)(2,1)}, u32[]{:S(2)}) %copy-start.7) | copy-done | bytes 8388632
  92.9 0.7 collective-permute-start.21
  93.6 0.7 collective-permute-start.20
  94.3 0.7 collective-permute-start.17
  95.0 0.7 collective-permute-start.19
  95.7 0.7 collective-permute-start.16
  96.3 1.3 collective-permute-start.18
  97.7 1.3 collective-permute-start.15
  99.0 2.4 %add_select_fusion = f32[1,32,8,1024]{3,2,1,0:T(8,128)} fusion(f32[1,32,8,1024]{3,2,1,0:T(8,128)} %param.21, f32[32,1024]{1,0:T(8,128)S(1)} %get-tuple-element.55, f32[32,1024]{1,0:T(8,128)S(1)} %get-tuple-element.54, f32[8,1024]{1,0:T(8,128)S(1)} %get-tuple-element.65, f32[8,1024]{1,0:T(8,128)S(1)} %get-tuple-element.64, pred[]{:T(512)S(6)} %eq.10), kind=kLoop, calls=%fused_computation.5 | loop fusion | flops 1835008 | bytes 2424833 | tf_op jit(solution)/shard_map/jit(_where)/select_n | solution.py:345
  101.4 56.4 %collective-permute-done.18 = bf16[16,2048]{1,0:T(8,128)(2,1)S(1)} collective-permute-done((bf16[16,2048]{1,0:T(8,128)(2,1)S(1)}, bf16[16,2048]{1,0:T(8,128)(2,1)S(1)}, u32[]{:S(2)}, u32[]{:S(2)}) %collective-permute-start.18) | collective-permute-done | bytes 65568 | tf_op jit(solution)/shard_map/ppermute | solution.py:312
  158.0 2.3 %fusion.3 = f32[1,32,6,1024]{3,1,2,0:T(8,128)} fusion(f32[32,6,1024]{2,0,1:T(8,128)} %bitcast.143, f32[32,2,1024]{2,0,1:T(8,128)S(1)} %bitcast.137, pred[]{:T(512)S(6)} %eq.10), kind=kLoop, calls=%fused_computation.8 | loop fusion | flops 393216 | bytes 1835009 | tf_op jit(solution)/shard_map/broadcast_in_dim | solution.py:349
  160.4 1.0 shard_map.159
  161.4 1.5 collective-permute-start.25
  162.9 0.6 collective-permute-start.24
  163.5 0.9 collective-permute-done.25
  164.4 2.1 %collective-permute-done.24 = f32[16,2]{1,0:T(8,128)S(1)} collective-permute-done((f32[16,2]{1,0:T(8,128)S(1)}, f32[16,2]{1,0:T(8,128)S(1)}, u32[]{:S(2)}, u32[]{:S(2)}) %collective-permute-start.24) | collective-permute-done | bytes 160 | tf_op jit(solution)/shard_map/ppermute | solution.py:335
  166.7 0.7 sub.32
  (86 shorter events, 4.5 us)
Async XLA Ops:
  0.6 1.2 copy-start
  0.6 28.9 %copy-start.10 = (f32[1,4096]{1,0:T(1,128)S(1)}, f32[1,4096]{1,0:T(1,128)}, u32[]{:S(2)}) copy-start(f32[1,4096]{1,0:T(1,128)} %gain.15) | copy-start | bytes 49156
  2.7 14.6 %collective-permute-start = (bf16[64,1024]{1,0:T(8,128)(2,1)S(1)}, bf16[64,1024]{1,0:T(8,128)(2,1)S(1)}, u32[]{:S(2)}, u32[]{:S(2)}) collective-permute-start(bf16[64,1024]{1,0:T(8,128)(2,1)S(1)} %broadcast_select_fusion), channel_id=1, source_target_pairs={{0,2},{1,3},{2,0},{3,1},{4,6},{5,7},{6,4},{7,5},{8,10},{9,11},{10,... | collective-permute-start | bytes 393224 | tf_op jit(solution)/shard_map/ppermute | solution.py:249
  17.5 12.1 %collective-permute-start.1 = (bf16[64,2048]{1,0:T(8,128)(2,1)S(1)}, bf16[64,2048]{1,0:T(8,128)(2,1)S(1)}, u32[]{:S(2)}, u32[]{:S(2)}) collective-permute-start(bf16[64,2048]{1,0:T(8,128)(2,1)S(1)} %pad_maximum_fusion.1.own), channel_id=1, source_target_pairs={{0,1},{1,0},{2,3},{3,2},{4,5},{5,4},{6,7},{7,6},{8,9},{9,8},{10,11... | collective-permute-start | bytes 786440 | tf_op jit(solution)/shard_map/ppermute | solution.py:183
  17.6 8.2 %copy-start.1 = (bf16[1,3,4096,1024]{3,2,1,0:T(8,128)(2,1)S(1)}, bf16[1,3,4096,1024]{3,2,1,0:T(8,128)(2,1)}, u32[]{:S(2)}) copy-start(bf16[1,3,4096,1024]{3,2,1,0:T(8,128)(2,1)} %param.14) | copy-start | bytes 75497472
  25.7 0.7 copy-start.9
  26.5 3.4 %copy-start.6 = (bf16[1,1024,4096]{2,1,0:T(8,128)(2,1)S(1)}, bf16[1,1024,4096]{2,1,0:T(8,128)(2,1)}, u32[]{:S(2)}) copy-start(bf16[1,1024,4096]{2,1,0:T(8,128)(2,1)} %param.15) | copy-start | bytes 25165828
  29.8 8.2 %copy-start.2 = (bf16[1,3,4096,1024]{3,2,1,0:T(8,128)(2,1)S(1)}, bf16[1,3,4096,1024]{3,2,1,0:T(8,128)(2,1)}, u32[]{:S(2)}) copy-start(bf16[1,3,4096,1024]{3,2,1,0:T(8,128)(2,1)} %param.14) | copy-start | bytes 75497472
  41.9 1.8 %collective-permute-start.2 = (bf16[64,2048]{1,0:T(8,128)(2,1)S(1)}, bf16[64,2048]{1,0:T(8,128)(2,1)S(1)}, u32[]{:S(2)}, u32[]{:S(2)}) collective-permute-start(bf16[64,2048]{1,0:T(8,128)(2,1)S(1)} %get-tuple-element.29), channel_id=1, source_target_pairs={{0,1},{1,0},{2,3},{3,2},{4,5},{5,4},{6,7},{7,6},{8,9},{9,8},{10,11... | collective-permute-start | bytes 786440 | tf_op jit(solution)/shard_map/ppermute | solution.py:183
  43.7 8.0 %collective-permute-start.4 = (bf16[64,2048]{1,0:T(8,128)(2,1)S(1)}, bf16[64,2048]{1,0:T(8,128)(2,1)S(1)}, u32[]{:S(2)}, u32[]{:S(2)}) collective-permute-start(bf16[64,2048]{1,0:T(8,128)(2,1)S(1)} %add_convert_fusion.6), channel_id=1, source_target_pairs={{0,6},{1,7},{2,4},{3,5},{16,22},{17,23},{18,20},{19,21}} | collective-permute-start | bytes 786440 | tf_op jit(solution)/shard_map/ppermute | solution.py:294
  45.1 11.9 %collective-permute-start.3 = (bf16[64,2048]{1,0:T(8,128)(2,1)S(1)}, bf16[64,2048]{1,0:T(8,128)(2,1)S(1)}, u32[]{:S(2)}, u32[]{:S(2)}) collective-permute-start(bf16[64,2048]{1,0:T(8,128)(2,1)S(1)} %add_convert_fusion.6), channel_id=1, source_target_pairs={{0,4},{1,5},{2,6},{3,7},{16,20},{17,21},{18,22},{19,23}} | collective-permute-start | bytes 786440 | tf_op jit(solution)/shard_map/ppermute | solution.py:294
  57.0 8.2 %collective-permute-start.5 = (bf16[64,2048]{1,0:T(8,128)(2,1)S(1)}, bf16[64,2048]{1,0:T(8,128)(2,1)S(1)}, u32[]{:S(2)}, u32[]{:S(2)}) collective-permute-start(bf16[64,2048]{1,0:T(8,128)(2,1)S(1)} %add_convert_fusion.5.own), channel_id=1, source_target_pairs={{0,1},{1,0},{2,3},{3,2},{4,5},{5,4},{6,7},{7,6},{8,9},{9,8},{10,11... | collective-permute-start | bytes 786440 | tf_op jit(solution)/shard_map/ppermute | solution.py:183
  57.1 8.2 %copy-start.3 = (bf16[1,3,4096,1024]{3,2,1,0:T(8,128)(2,1)S(1)}, bf16[1,3,4096,1024]{3,2,1,0:T(8,128)(2,1)}, u32[]{:S(2)}) copy-start(bf16[1,3,4096,1024]{3,2,1,0:T(8,128)(2,1)} %param.14) | copy-start | bytes 75497472
  65.3 1.7 collective-permute-start.6
  67.0 1.4 collective-permute-start.8
  67.7 0.7 collective-permute-start.7
  68.5 8.6 %collective-permute-start.9 = (bf16[64,2048]{1,0:T(8,128)(2,1)S(1)}, bf16[64,2048]{1,0:T(8,128)(2,1)S(1)}, u32[]{:S(2)}, u32[]{:S(2)}) collective-permute-start(bf16[64,2048]{1,0:T(8,128)(2,1)S(1)} %add_convert_fusion.3.own), channel_id=1, source_target_pairs={{0,1},{1,0},{2,3},{3,2},{4,5},{5,4},{6,7},{7,6},{8,9},{9,8},{10,11... | collective-permute-start | bytes 786440 | tf_op jit(solution)/shard_map/ppermute | solution.py:183
  68.9 8.2 %copy-start.4 = (bf16[1,3,4096,1024]{3,2,1,0:T(8,128)(2,1)S(1)}, bf16[1,3,4096,1024]{3,2,1,0:T(8,128)(2,1)}, u32[]{:S(2)}) copy-start(bf16[1,3,4096,1024]{3,2,1,0:T(8,128)(2,1)} %param.14) | copy-start | bytes 75497472
  77.1 1.5 collective-permute-start.10
  78.8 1.4 collective-permute-start.12
  79.4 0.7 collective-permute-start.11
  80.2 8.4 %collective-permute-start.13 = (bf16[64,2048]{1,0:T(8,128)(2,1)S(1)}, bf16[64,2048]{1,0:T(8,128)(2,1)S(1)}, u32[]{:S(2)}, u32[]{:S(2)}) collective-permute-start(bf16[64,2048]{1,0:T(8,128)(2,1)S(1)} %add_convert_fusion.1.own), channel_id=1, source_target_pairs={{0,1},{1,0},{2,3},{3,2},{4,5},{5,4},{6,7},{7,6},{8,9},{9,8},{10,11... | collective-permute-start | bytes 786440 | tf_op jit(solution)/shard_map/ppermute | solution.py:183
  80.4 8.2 %copy-start.5 = (bf16[1,3,4096,1024]{3,2,1,0:T(8,128)(2,1)S(1)}, bf16[1,3,4096,1024]{3,2,1,0:T(8,128)(2,1)}, u32[]{:S(2)}) copy-start(bf16[1,3,4096,1024]{3,2,1,0:T(8,128)(2,1)} %param.14) | copy-start | bytes 75497472
  88.6 0.7 copy-start.12
  88.6 71.8 %copy-start.8 = (bf16[4096,128]{1,0:T(8,128)(2,1)S(1)}, bf16[4096,128]{1,0:T(8,128)(2,1)}, u32[]{:S(2)}) copy-start(bf16[4096,128]{1,0:T(8,128)(2,1)} %unembed.1) | copy-start | bytes 3145732
  88.6 71.8 %copy-start.11 = (f32[4096]{0:T(1024)S(1)}, f32[4096]{0:T(1024)}, u32[]{:S(2)}) copy-start(f32[4096]{0:T(1024)} %param.22) | copy-start | bytes 49156
  88.6 4.2 %collective-permute-start.14 = (bf16[64,2048]{1,0:T(8,128)(2,1)S(1)}, bf16[64,2048]{1,0:T(8,128)(2,1)S(1)}, u32[]{:S(2)}, u32[]{:S(2)}) collective-permute-start(bf16[64,2048]{1,0:T(8,128)(2,1)S(1)} %get-tuple-element.44), channel_id=1, source_target_pairs={{0,1},{1,0},{2,3},{3,2},{4,5},{5,4},{6,7},{7,6},{8,9},{9,8},{10,11... | collective-permute-start | bytes 786440 | tf_op jit(solution)/shard_map/ppermute | solution.py:183
  89.4 3.4 %copy-start.7 = (bf16[1,1024,4096]{2,1,0:T(8,128)(2,1)S(1)}, bf16[1,1024,4096]{2,1,0:T(8,128)(2,1)}, u32[]{:S(2)}) copy-start(bf16[1,1024,4096]{2,1,0:T(8,128)(2,1)} %param.15) | copy-start | bytes 25165828
  92.9 3.4 %collective-permute-start.21 = (bf16[16,2048]{1,0:T(8,128)(2,1)S(1)}, bf16[16,2048]{1,0:T(8,128)(2,1)S(1)}, u32[]{:S(2)}, u32[]{:S(2)}) collective-permute-start(bf16[16,2048]{1,0:T(8,128)(2,1)S(1)} %get-tuple-element.59), channel_id=1, source_target_pairs={{12,14},{13,15},{14,12},{15,13},{28,30},{29,31},{30,28},{31,29}} | collective-permute-start | bytes 196616 | tf_op jit(solution)/shard_map/ppermute | solution.py:312
  93.6 4.0 %collective-permute-start.20 = (bf16[16,2048]{1,0:T(8,128)(2,1)S(1)}, bf16[16,2048]{1,0:T(8,128)(2,1)S(1)}, u32[]{:S(2)}, u32[]{:S(2)}) collective-permute-start(bf16[16,2048]{1,0:T(8,128)(2,1)S(1)} %get-tuple-element.57), channel_id=1, source_target_pairs={{12,10},{13,11},{14,8},{15,9},{28,26},{29,27},{30,24},{31,25}} | collective-permute-start | bytes 196616 | tf_op jit(solution)/shard_map/ppermute | solution.py:312
  94.3 63.5 %collective-permute-start.17 = (bf16[16,2048]{1,0:T(8,128)(2,1)S(1)}, bf16[16,2048]{1,0:T(8,128)(2,1)S(1)}, u32[]{:S(2)}, u32[]{:S(2)}) collective-permute-start(bf16[16,2048]{1,0:T(8,128)(2,1)S(1)} %get-tuple-element.57), channel_id=1, source_target_pairs={{12,8},{13,9},{14,10},{15,11},{28,24},{29,25},{30,26},{31,27}} | collective-permute-start | bytes 196616 | tf_op jit(solution)/shard_map/ppermute | solution.py:312
  95.0 6.4 %collective-permute-start.19 = (bf16[16,2048]{1,0:T(8,128)(2,1)S(1)}, bf16[16,2048]{1,0:T(8,128)(2,1)S(1)}, u32[]{:S(2)}, u32[]{:S(2)}) collective-permute-start(bf16[16,2048]{1,0:T(8,128)(2,1)S(1)} %get-tuple-element.58), channel_id=1, source_target_pairs={{12,6},{13,7},{14,4},{15,5},{28,22},{29,23},{30,20},{31,21}} | collective-permute-start | bytes 196616 | tf_op jit(solution)/shard_map/ppermute | solution.py:312
  95.7 62.2 %collective-permute-start.16 = (bf16[16,2048]{1,0:T(8,128)(2,1)S(1)}, bf16[16,2048]{1,0:T(8,128)(2,1)S(1)}, u32[]{:S(2)}, u32[]{:S(2)}) collective-permute-start(bf16[16,2048]{1,0:T(8,128)(2,1)S(1)} %get-tuple-element.58), channel_id=1, source_target_pairs={{12,4},{13,5},{14,6},{15,7},{28,20},{29,21},{30,22},{31,23}} | collective-permute-start | bytes 196616 | tf_op jit(solution)/shard_map/ppermute | solution.py:312
  96.3 61.5 %collective-permute-start.18 = (bf16[16,2048]{1,0:T(8,128)(2,1)S(1)}, bf16[16,2048]{1,0:T(8,128)(2,1)S(1)}, u32[]{:S(2)}, u32[]{:S(2)}) collective-permute-start(bf16[16,2048]{1,0:T(8,128)(2,1)S(1)} %get-tuple-element.56), channel_id=1, source_target_pairs={{12,2},{13,3},{14,0},{15,1},{28,18},{29,19},{30,16},{31,17}} | collective-permute-start | bytes 196616 | tf_op jit(solution)/shard_map/ppermute | solution.py:312
  97.7 60.2 %collective-permute-start.15 = (bf16[16,2048]{1,0:T(8,128)(2,1)S(1)}, bf16[16,2048]{1,0:T(8,128)(2,1)S(1)}, u32[]{:S(2)}, u32[]{:S(2)}) collective-permute-start(bf16[16,2048]{1,0:T(8,128)(2,1)S(1)} %get-tuple-element.56), channel_id=1, source_target_pairs={{12,0},{13,1},{14,2},{15,3},{28,16},{29,17},{30,18},{31,19}} | collective-permute-start | bytes 196616 | tf_op jit(solution)/shard_map/ppermute | solution.py:312
  157.9 2.4 %collective-permute-start.22 = (bf16[16,2048]{1,0:T(8,128)(2,1)S(1)}, bf16[16,2048]{1,0:T(8,128)(2,1)S(1)}, u32[]{:S(2)}, u32[]{:S(2)}) collective-permute-start(bf16[16,2048]{1,0:T(8,128)(2,1)S(1)} %add_convert_fusion.7.own), channel_id=1, source_target_pairs={{0,1},{1,0},{2,3},{3,2},{4,5},{5,4},{6,7},{7,6},{8,9},{9,8},{10,11... | collective-permute-start | bytes 196616 | tf_op jit(solution)/shard_map/ppermute | solution.py:183
  161.4 3.1 %collective-permute-start.25 = (f32[16,2]{1,0:T(8,128)S(1)}, f32[16,2]{1,0:T(8,128)S(1)}, u32[]{:S(2)}, u32[]{:S(2)}) collective-permute-start(f32[16,2]{1,0:T(8,128)S(1)} %bitcast.139), channel_id=1, source_target_pairs={{0,3},{1,2},{2,1},{3,0},{4,7},{5,6},{6,5},{7,4},{8,11},{9,10},{10,... | collective-permute-start | bytes 392 | tf_op jit(solution)/shard_map/ppermute | solution.py:335
  162.9 3.7 %collective-permute-start.24 = (f32[16,2]{1,0:T(8,128)S(1)}, f32[16,2]{1,0:T(8,128)S(1)}, u32[]{:S(2)}, u32[]{:S(2)}) collective-permute-start(f32[16,2]{1,0:T(8,128)S(1)} %bitcast.140), channel_id=1, source_target_pairs={{0,2},{1,3},{2,0},{3,1},{4,6},{5,7},{6,4},{7,5},{8,10},{9,11},{10,... | collective-permute-start | bytes 392 | tf_op jit(solution)/shard_map/ppermute | solution.py:335
  163.5 3.1 %collective-permute-start.23 = (f32[16,2]{1,0:T(8,128)S(1)}, f32[16,2]{1,0:T(8,128)S(1)}, u32[]{:S(2)}, u32[]{:S(2)}) collective-permute-start(f32[16,2]{1,0:T(8,128)S(1)} %bitcast.141), channel_id=1, source_target_pairs={{0,1},{1,0},{2,3},{3,2},{4,5},{5,4},{6,7},{7,6},{8,9},{9,8},{10,11... | collective-permute-start | bytes 392 | tf_op jit(solution)/shard_map/ppermute | solution.py:335

commit v2 on v1

v2 whole, which is shorter than its diff:
```python
import functools

import jax
import jax.numpy as jnp
from jax import lax
from jax.experimental import pallas as pl
from jax.experimental.pallas import tpu as pltpu
from jax.sharding import PartitionSpec as P

EPS = 1e-05
BOTH = ("segment", "inner")
VM = pl.BlockSpec(memory_space=pltpu.VMEM)


ANY = pl.BlockSpec(memory_space=pl.ANY)


def in_kernel_memory(array):
    return pltpu.with_memory_space_constraint(array, pltpu.VMEM)


def in_main_memory(array):
    return pltpu.with_memory_space_constraint(array, pltpu.HBM)


def load_copies(source, target, semaphores):
    rows = source.shape[-2]
    count = semaphores.shape[0]
    size = rows // count
    copies = []
    for place in range(count):
        part = slice(place * size, (place + 1) * size)
        index = (slice(None),) * (len(source.shape) - 2) + (part, slice(None))
        copies.append(
            pltpu.make_async_copy(source.at[index], target.at[index], semaphores.at[place])
        )
    return copies


def lanes(index, width):
    return pl.ds(pl.multiple_of(index * width, width), width)


def column_tile(width):
    return min(512, width)


def dot(left, right):
    return jnp.dot(left, right, preferred_element_type=jnp.float32)


def take(refs, place, width):
    if len(refs) == 1:
        return refs[0][:, place * width : (place + 1) * width]
    return refs[place][...]


def chip_at(refs, place, chips):
    if len(refs) == 1:
        return place
    return lax.rem(lax.div(lax.axis_index("inner"), 2) - place + chips, chips)


def scaled_half(refs, gain_ref, scaled, core, chips, width):
    total = None
    for place in range(chips):
        values = take(refs, place, width).astype(jnp.float32)
        part = jnp.sum(values * values, axis=-1, keepdims=True)
        total = part if total is None else total + part
        gain = gain_ref[:, lanes(2 * chip_at(refs, place, chips) + core, width)]
        scaled[:, place * width : (place + 1) * width] = (values * gain).astype(jnp.bfloat16)
    return total


def half_product(refs, scaled, w_in, part, core, columns, chips, width):
    total = None
    for place in range(chips):
        rows = lanes(2 * chip_at(refs, place, chips) + core, width)
        term = dot(scaled[:, place * width : (place + 1) * width], w_in[part, rows, columns])
        total = term if total is None else total + term
    return total


def first_kernel(stage, chips, pieces, *refs):
    own, refs = refs[:pieces], refs[pieces:]
    copies = []
    if stage == 0:
        gain, w_in, w_out, sums, squares, w_held, scaled, semaphores = refs
        copies = load_copies(w_out, w_held, semaphores)
    else:
        gain, w_in, sums, squares, scaled = refs
    for copy in copies:
        copy.start()
    width = w_in.shape[2]
    tile = column_tile(width)

    @pl.when(lax.axis_index("segment") == stage)
    def _():
        core = lax.rem(lax.axis_index("inner"), 2)
        total = scaled_half(own, gain, scaled, core, chips, width)
        squares[...] = jnp.broadcast_to(total, squares.shape)
        for part in range(3):

            @pl.loop(0, width // tile)
            def _(step):
                columns = lanes(step, tile)
                sums[part, :, columns] = half_product(
                    own, scaled, w_in, part, core, columns, chips, width
                )

    for copy in copies:
        copy.wait()


def second_kernel(stage, chips, steps, pieces, *refs):
    other, refs = refs[:pieces], refs[pieces:]
    gain, w_in, sums, squares, fixed, factors, _, w_out = refs[:8]
    product, gated, partner, scaled = refs[8:]
    width = w_in.shape[2]
    tile = column_tile(width)
    seqs = gated.shape[0] // steps
    features = w_in.shape[1]

    @pl.when(lax.axis_index("segment") == stage)
    def _():
        core = lax.rem(lax.axis_index("inner"), 2)
        facing = 1 - core
        total = scaled_half(other, gain, scaled, facing, chips, width)
        mean_square = (total + squares[:, :1]) / features
        scale = lax.rsqrt(mean_square + EPS)

        @pl.loop(0, width // tile)
        def _(step):
            columns = lanes(step, tile)
            query, key, value = (
                scale
                * (
                    sums[part, :, columns]
                    + half_product(other, scaled, w_in, part, facing, columns, chips, width)
                )
                for part in range(3)
            )
            entry = key * value
            product[:, columns] = entry
            for now in range(steps):
                rows = slice(now * seqs, (now + 1) * seqs)
                filtered = fixed[now, :, columns]
                for back in range(now + 1):
                    source = slice((now - back) * seqs, (now - back + 1) * seqs)
                    filtered = filtered + factors[back : back + 1, columns] * entry[source]
                gated[rows, columns] = (query[rows] * filtered).astype(jnp.bfloat16)

        for chip in range(chips):
            out_piece(gated, w_out, partner, chip, facing, chips, None)


def out_piece(gated, w_out, result, chip, core, chips, share):
    width = w_out.shape[1] // (2 * chips)
    tile = column_tile(width)

    @pl.loop(0, width // tile)
    def _(step):
        source = pl.ds(pl.multiple_of((2 * chip + core) * width + step * tile, tile), tile)
        target = pl.ds(pl.multiple_of(chip * width + step * tile, tile), tile)
        value = dot(gated[...], w_out[:, source])
        if share is not None:
            ref, offset = share
            columns = pl.ds(pl.multiple_of(offset + step * tile, tile), tile)
            value = value + ref[:, columns].astype(jnp.float32) * (1.0 / chips)
        result[:, target] = value.astype(result.dtype)


def third_kernel(stage, chips, pieces, *refs):
    own, (gated, w_out, result) = refs[:pieces], refs[pieces:]
    width = w_out.shape[1] // (2 * chips)

    @pl.when(lax.axis_index("segment") == stage)
    def _():
        core = lax.rem(lax.axis_index("inner"), 2)
        for place in range(chips):
            share = (own[0], place * width) if pieces == 1 else (own[place], 0)
            out_piece(gated, w_out, result, chip_at(own, place, chips), core, chips, share)


def pick_kernel(tokens, embedding, picked):
    steps, seqs = tokens.shape[0] - 1, tokens.shape[1]
    places = lax.broadcasted_iota(jnp.int32, (embedding.shape[0], seqs), 0)
    for now in range(steps):
        chosen = jnp.where(places == tokens[now : now + 1, :], 1.0, 0.0).astype(jnp.bfloat16)
        rows = lax.dot_general(
            chosen, embedding[...], (((0,), (0,)), ((), ())), preferred_element_type=jnp.float32
        )
        picked[now * seqs : (now + 1) * seqs, :] = rows.astype(jnp.bfloat16)


def prepare_kernel(
    fir, modal, taps, rate, residue, w_in, fixed, factors, product, w_held, semaphores
):
    copies = load_copies(w_in, w_held, semaphores)
    for copy in copies:
        copy.start()
    steps = fixed.shape[0]
    held = fir.shape[0]
    is_short = lax.rem(lax.axis_index("segment"), 2) == 0
    product[...] = jnp.zeros_like(product)

    @pl.when(is_short)
    def _():
        for now in range(steps):
            factors[now : now + 1, :] = taps[now]
            total = None
            for place in range(now, held):
                term = fir[place] * taps[held + now - place]
                total = term if total is None else total + term
            fixed[now] = total

    @pl.when(jnp.logical_not(is_short))
    def _():
        decay = jnp.exp(-rate[...])
        power = residue[...]
        for now in range(steps):
            factor = jnp.sum(power * (1.0 - decay), axis=0, keepdims=True)
            factors[now : now + 1, :] = factor + taps[0] if now == 0 else factor
            power = power * decay
            fixed[now] = jnp.sum(modal[...] * power[None], axis=1)

    for copy in copies:
        copy.wait()


def call(kernel, outs, args, scratch=(), aliases=None, specs=None, flops=0, nbytes=0):
    return pl.pallas_call(
        kernel,
        out_shape=outs,
        in_specs=specs or [VM] * len(args),
        out_specs=jax.tree.map(lambda _: VM, outs),
        scratch_shapes=scratch,
        input_output_aliases=aliases or {},
        compiler_params=pltpu.CompilerParams(vmem_limit_bytes=4 << 20),
        cost_estimate=pl.CostEstimate(flops=flops, bytes_accessed=nbytes, transcendentals=0),
    )(*args)


def join_kernel(*refs):
    terms, result = refs[:-1], refs[-1]
    total = terms[0][...].astype(jnp.float32)
    for term in terms[1:]:
        total = total + term[...].astype(jnp.float32)
    result[...] = total.astype(result.dtype)


def spread_kernel(steps, mine, facing, *blocks):
    seqs = mine.shape[0] // steps
    size = seqs // len(blocks)
    for place, block in enumerate(blocks):
        for now in range(steps):
            rows = slice(now * seqs + place * size, now * seqs + (place + 1) * size)
            value = mine[rows, :] + facing[rows, :].astype(jnp.float32)
            block[now * size : (now + 1) * size, :] = value.astype(block.dtype)


def collect_kernel(stage, kept, *refs):
    arrived, (_, result) = refs[:-2], refs[-2:]
    here = lax.axis_index("segment")
    for place, ref in enumerate((*arrived, kept)):

        @pl.when(here == place)
        def _():
            result[...] = ref[...]


def state_kernel(product, fir, modal, rate, fir_out, modal_out, token):
    held, seqs, width = fir.shape
    steps = product.shape[0] // seqs
    is_short = lax.rem(lax.axis_index("segment"), 2) == 0
    token[...] = jnp.zeros_like(token)

    @pl.when(is_short)
    def _():
        modal_out[...] = modal[...]
        fir_out[: held - steps] = fir[steps:]
        for now in range(steps):
            fir_out[held - steps + now] = product[now * seqs : (now + 1) * seqs, :]

    @pl.when(jnp.logical_not(is_short))
    def _():
        fir_out[...] = fir[...]
        decay = jnp.exp(-rate[...])[None]
        values = modal[...]
        for now in range(steps):
            entry = product[now * seqs : (now + 1) * seqs, :]
            values = decay * values + (1.0 - decay) * entry[:, None, :]
        modal_out[...] = values


def head_kernel(chips, own, other, gain, unembed, tokens, logits, sums, head_in):
    steps, block, vocab = logits.shape
    width = gain.shape[1] // (2 * chips)
    inner = lax.axis_index("inner")
    segment = lax.axis_index("segment")
    core = lax.rem(inner, 2)
    total = jnp.zeros((own.shape[0], 1), jnp.float32)
    for half_ref in (own, other):
        values = half_ref[...].astype(jnp.float32)
        total = total + jnp.sum(values * values, axis=-1, keepdims=True)
    scale = lax.rsqrt(total / gain.shape[1] + EPS)
    for half_ref, which in ((own, core), (other, 1 - core)):
        for chip in range(chips):
            values = half_ref[:, chip * width : (chip + 1) * width].astype(jnp.float32)
            place = lanes(2 * chip + which, width)
            head_in[:, place] = (values * scale * gain[:, place]).astype(jnp.bfloat16)
    result = dot(head_in[...], unembed[...])
    row = lax.broadcasted_iota(jnp.int32, result.shape, 0)
    column = lax.broadcasted_iota(jnp.int32, result.shape, 1) + inner * vocab
    wanted = jnp.full(result.shape, -1, jnp.int32)
    for now in range(steps):
        logits[now] = result[now * block : (now + 1) * block, :]
        for place in range(block):
            wanted = jnp.where(
                row == now * block + place, tokens[now + 1, segment * block + place], wanted
            )
    exp_local = jnp.sum(jnp.exp(result), axis=-1, keepdims=True)
    chosen = jnp.where(column == wanted, result, 0.0)
    target_local = jnp.sum(chosen, axis=-1, keepdims=True)
    place = lax.broadcasted_iota(jnp.int32, sums.shape, 1)
    sums[...] = jnp.where(place == 0, exp_local, target_local)


def total_kernel(*refs):
    parts, result = refs[:-1], refs[-1]
    steps, block = result.shape
    total = parts[0][...]
    for part in parts[1:]:
        total = total + part[...]
    column = total[:, 1:2] - jnp.log(total[:, :1])
    down = lax.broadcasted_iota(jnp.int32, (block, block), 0)
    along = lax.broadcasted_iota(jnp.int32, (block, block), 1)
    for now in range(steps):
        spread = jnp.where(down == along, column[now * block : (now + 1) * block, :], 0.0)
        result[now : now + 1, :] = jnp.sum(spread, axis=0, keepdims=True)


def swap_cores(block):
    count = lax.axis_size("inner")
    return lax.ppermute(block, "inner", [(i, i ^ 1) for i in range(count)])


def hop_chips(block, hop):
    count = lax.axis_size("inner")
    return lax.ppermute(block, "inner", [(i, (i + 2 * hop) % count) for i in range(count)])


def per_device(
    tokens,
    embedding,
    in_proj,
    out_proj,
    norm_gain,
    fir_taps,
    modal_rate,
    modal_residue,
    fir_state,
    modal_state,
    final_gain,
    unembed,
):
    segments = lax.axis_size("segment")
    count = lax.axis_size("inner")
    chips = count // 2
    steps = tokens.shape[0] - 1
    seqs = tokens.shape[1]
    rows = steps * seqs
    width = embedding.shape[1]
    half = chips * width
    features = half * 2
    f32, bf16 = jnp.float32, jnp.bfloat16
    shape = jax.ShapeDtypeStruct
    w_in = in_main_memory(in_proj[0])
    w_out = in_main_memory(out_proj[0])
    taps = fir_taps.transpose(1, 0, 2)
    rate, residue = modal_rate[0], modal_residue[0]
    fir, modal = fir_state[0].transpose(1, 0, 2), modal_state[0]

    picked = call(
        pick_kernel,
        shape((rows, width), bf16),
        (tokens, embedding),
        flops=2 * rows * width * embedding.shape[0],
        nbytes=2 * width * embedding.shape[0],
    )
    own = [hop_chips(picked, hop) if hop else picked for hop in range(chips)]
    fixed, factors, product, w_in = call(
        prepare_kernel,
        (
            shape((steps, seqs, width), f32),
            shape((steps, width), f32),
            shape((rows, width), f32),
            pltpu.VMEM(w_in.shape, bf16),
        ),
        (fir, modal, taps, rate, residue, w_in),
        specs=[VM] * 5 + [ANY],
        scratch=[pltpu.SemaphoreType.DMA((8,))],
        flops=8 * seqs * width * steps,
        nbytes=64 * seqs * width,
    )

    for stage in range(segments):
        pieces = len(own)
        other = [swap_cores(piece) for piece in own]
        outs = (shape((3, rows, width), f32), shape((rows, 128), f32))
        args = (*own, norm_gain, w_in)
        scratch = [pltpu.VMEM((rows, half), bf16)]
        specs = [VM] * len(args)
        if stage == 0:
            outs += (pltpu.VMEM(w_out.shape, bf16),)
            args += (w_out,)
            specs += [ANY]
            scratch += [pltpu.SemaphoreType.DMA((4,))]
        sums, squares, *held = call(
            functools.partial(first_kernel, stage, chips, pieces),
            outs,
            args,
            specs=specs,
            scratch=scratch,
            flops=6 * rows * half * width,
            nbytes=6 * half * width,
        )
        w_out = held[0] if held else w_out
        product, gated, partner = call(
            functools.partial(second_kernel, stage, chips, steps, pieces),
            (shape((rows, width), f32), shape((rows, width), bf16), shape((rows, half), bf16)),
            (*other, norm_gain, w_in, sums, squares, fixed, factors, product, w_out),
            scratch=[pltpu.VMEM((rows, half), bf16)],
            aliases={pieces + 6: 0},
            flops=8 * rows * half * width,
            nbytes=8 * half * width,
        )
        facing = swap_cores(partner)
        mine = call(
            functools.partial(third_kernel, stage, chips, pieces),
            shape((rows, half), f32),
            (*own, gated, w_out),
            flops=2 * rows * half * width,
            nbytes=2 * half * width,
        )
        if stage < segments - 1:
            chip_sum = call(join_kernel, shape((rows, half), bf16), (mine, facing))
            terms = []
            for hop in range(chips):
                route = [
                    (stage * count + i, (stage + 1) * count + (i + 2 * hop) % count)
                    for i in range(count)
                ]
                terms.append(lax.ppermute(chip_sum, BOTH, route))
            own = [call(join_kernel, shape((rows, half), bf16), terms)]

    block = seqs // segments
    last = segments - 1
    head_rows = steps * block
    piece = shape((head_rows, half), bf16)
    blocks = call(functools.partial(spread_kernel, steps), (piece,) * segments, (mine, facing))
    arrived = [lax.ppermute(blocks[k], "segment", [(last, k)]) for k in range(last)]
    fir_out, modal_out, token = call(
        state_kernel,
        (shape(fir.shape, f32), shape(modal.shape, f32), shape((8, 128), f32)),
        (product, fir, modal, rate),
        nbytes=8 * seqs * width * 14,
    )
    part = call(
        functools.partial(collect_kernel, last), piece, (blocks[last], *arrived, token)
    )
    hops = [hop_chips(part, hop) for hop in range(1, chips)]
    own = call(join_kernel, piece, (part, *hops))
    other = swap_cores(own)
    vocab = unembed.shape[1]
    logits, totals = call(
        functools.partial(head_kernel, chips),
        (shape((steps, block, vocab), f32), shape((head_rows, 128), f32)),
        (own, other, final_gain[None], in_kernel_memory(unembed), tokens),
        specs=[VM] * 4 + [pl.BlockSpec(memory_space=pltpu.SMEM)],
        scratch=[pltpu.VMEM((head_rows, features), bf16)],
        flops=2 * head_rows * features * vocab,
        nbytes=2 * features * vocab,
    )
    parts = [totals]
    for hop in range(1, count):
        route = [(i, (i + hop) % count) for i in range(count)]
        parts.append(lax.ppermute(totals, "inner", route))
    logprob = call(total_kernel, shape((steps, block), f32), parts)
    return logits, logprob, fir_out.transpose(1, 0, 2)[None], modal_out[None]


def solution(mesh):
    return jax.shard_map(
        per_device,
        mesh=mesh,
        in_specs=(
            P(None, "groups"),
            P(None, "inner"),
            P("segment", None, None, "inner"),
            P("segment", "inner", None),
            P("segment", None),
            P("segment", None, "inner"),
            P("segment", None, "inner"),
            P("segment", None, "inner"),
            P("segment", "groups", None, "inner"),
            P("segment", "groups", None, "inner"),
            P(),
            P(None, "inner"),
        ),
        out_specs=(
            P(None, ("groups", "segment"), "inner"),
            P(None, ("groups", "segment")),
            P("segment", "groups", None, "inner"),
            P("segment", "groups", None, "inner"),
        ),
        check_vma=False,
    )
```

time: 168 us -> 122 us (0.73)
  local copies, waits for them, and re-layouts: 50.2 us -> 6.55 us
  Pallas kernels: 9.13 us -> 21.5 us
  other arithmetic: 11.5 us -> 0 us
  between operations: 5.01 us -> 0.95 us
  waiting for transfers between devices: 72.7 us -> 76.7 us
  starting transfers between devices: 18.9 us -> 16.3 us
    unnamed x26 -> x28, local copies, waits for them, and re-layouts: 45.6 us -> 6.55 us
    pallas_call x13 -> x26, Pallas kernels: 9.13 us -> 21.5 us  [call(): pl.pallas_call(kernel, out_shape=outs, in_specs=specs or [VM] * len(args)...]
    ppermute x9 -> x10, waiting for transfers between devices: 2.58 us -> 9.69 us  [swap_cores(): return lax.ppermute(block, 'inner', [(i, i ^ 1) for i in range(count)])]
    ppermute x17 -> x14, waiting for transfers between devices: 70.1 us -> 67 us  [the longest x3 47.2 us: per_device(): lax.ppermute(blocks[k], 'segment', [(last, k)])]
    slice x5 -> x0, local copies, waits for them, and re-layouts: 2.85 us -> none  [the longest x1 0.78 us: short_parts(): total = total + fir[:, held - (back - now)] * taps[back]]
    reduce_sum x2 -> x0, other arithmetic: 2.68 us -> none  [the longest x1 1.88 us: modal_parts(): fixed.append(jnp.sum((residue * power)[None] * modal, axis=1))]
    select_n x7 -> x0, other arithmetic: 2.66 us -> none  [the longest x1 2.44 us: per_device(): modal_out = jnp.where(is_short, modal, modal_next)]
    broadcast_in_dim x1 -> x0, other arithmetic: 2.28 us -> none  [per_device(): fir_out[None]]
  transfers between devices with their start and end apart: 26 -> 24, of which waited for: 7 -> 14; matrix products, arithmetic and copies ran while one was open for 8% -> 0% of each run, Pallas kernels for 3% -> 12%
where the time goes in v2:
time: 122 us
  waiting for transfers between devices  76.7 us (63%)
  Pallas kernels  21.5 us (18%)
  starting transfers between devices  16.3 us (13%)
  local copies, waits for them, and re-layouts  6.55 us (5%)
    ppermute x3, waiting for transfers between devices, per_device(): lax.ppermute(blocks[k], 'segment', [(last, k)])  47.2 us
    pallas_call x26, Pallas kernels, call(): pl.pallas_call(kernel, out_shape=outs, in_specs=specs or [VM] * len(args)...  21.5 us
    ppermute x6, waiting for transfers between devices, per_device(): terms.append(lax.ppermute(chip_sum, BOTH, route))  10.6 us
    ppermute x10, waiting for transfers between devices, swap_cores(): return lax.ppermute(block, 'inner', [(i, i ^ 1) for i in range(count)])  9.69 us
    unnamed x28, local copies, waits for them, and re-layouts  6.55 us
    ppermute x2, waiting for transfers between devices, hop_chips(): lax.ppermute(block, 'inner', [(i, (i + 2 * hop) % count) for i in range(c...  6.02 us
    ppermute x6, starting transfers between devices, per_device(): terms.append(lax.ppermute(chip_sum, BOTH, route))  5.32 us
    ppermute x2, starting transfers between devices, hop_chips(): lax.ppermute(block, 'inner', [(i, (i + 2 * hop) % count) for i in range(c...  4.81 us
  transfers between devices with their start and end apart: 24, of which 14 were waited for; matrix products, arithmetic and copies ran while one was open for 0% of the time, Pallas kernels for 12%

profile of v2, /device:TPU:0, one launch (start us, length us, event | category | flops | bytes accessed | tf_op | source)
XLA Modules:
  0.0 121.9 jit_solution(10083278536813836972)
XLA Ops:
  0.6 1.2 copy-done.4
  1.9 0.7 copy-done.12
  2.5 0.5 shard_map.147.refs_0_
  3.0 3.0 %collective-permute-start = (bf16[64,1024]{1,0:T(8,128)(2,1)S(1)}, bf16[64,1024]{1,0:T(8,128)(2,1)S(1)}, u32[]{:S(2)}, u32[]{:S(2)}) collective-permute-start(bf16[64,1024]{1,0:T(8,128)(2,1)S(1)} %shard_map.147.refs_0_), channel_id=1, source_target_pairs={{0,2},{1,3},{2,0},{3,1},{4,6},{5,7},{6,4},{7,5},{8,10},{9,11},{10,... | collective-permute-start | bytes 393224 | tf_op jit(solution)/shard_map/ppermute | solution.py:350
  6.0 3.5 %collective-permute-done.refs_1_ = bf16[64,1024]{1,0:T(8,128)(2,1)S(1)} collective-permute-done((bf16[64,1024]{1,0:T(8,128)(2,1)S(1)}, bf16[64,1024]{1,0:T(8,128)(2,1)S(1)}, u32[]{:S(2)}, u32[]{:S(2)}) %collective-permute-start) | collective-permute-done | bytes 131104 | tf_op jit(solution)/shard_map/ppermute | solution.py:350
  9.5 1.2 %copy-done = f32[1,32,8,1024]{3,2,1,0:T(8,128)S(1)} copy-done((f32[1,32,8,1024]{3,2,1,0:T(8,128)S(1)}, f32[1,32,8,1024]{3,2,1,0:T(8,128)}, u32[]{:S(2)}) %copy-start) | copy-done | bytes 1048600
  10.8 1.1 copy-done.2
  11.9 0.8 copy-done.7
  12.7 0.8 copy-done.9
  13.4 0.7 copy-done.10
  14.2 8.3 %shard_map.148 = (f32[2,32,1024]{2,1,0:T(8,128)S(1)}, f32[2,1024]{1,0:T(2,128)S(1)}, f32[64,1024]{1,0:T(8,128)S(1)}, bf16[3,4096,1024]{2,1,0:T(8,128)(2,1)S(1)}) custom-call(f32[6,32,1024]{2,1,0:T(8,128)S(1)} %bitcast.16, f32[32,8,1024]{2,1,0:T(8,128)S(1)} %bitcast.14, f32[7,1,1024]{2,1,0:T(1,128)S(1)} %bitcast.21, f32[8,1024]{1,0:T(8,128)S(1)} %bitcast.18, ...), custom_call_target="tpu_custom_call" | custom-call | flops 524288 | bytes 2097152 | tf_op jit(solution)/shard_map/pallas_call | solution.py:232
  22.5 3.5 %shard_map.149 = (f32[3,64,1024]{2,1,0:T(8,128)S(1)}, f32[64,128]{1,0:T(8,128)S(1)}, bf16[1024,4096]{1,0:T(8,128)(2,1)S(1)}) custom-call(bf16[64,1024]{1,0:T(8,128)(2,1)S(1)} %shard_map.147.refs_0_, bf16[64,1024]{1,0:T(8,128)(2,1)S(1)} %collective-permute-done.refs_1_, f32[1,4096]{1,0:T(1,128)S(1)} %copy-done.6, ...), custom_call_target="tpu_custom_call" | custom-call | flops 805306368 | bytes 12582912 | tf_op jit(solution)/shard_map/pallas_call | solution.py:232
  26.0 3.9 %shard_map.150 = (f32[64,1024]{1,0:T(8,128)S(1)}, bf16[64,1024]{1,0:T(8,128)(2,1)S(1)}, bf16[64,2048]{1,0:T(8,128)(2,1)S(1)}) custom-call(bf16[64,1024]{1,0:T(8,128)(2,1)S(1)} %collective-permute-done.1.refs_0_, bf16[64,1024]{1,0:T(8,128)(2,1)S(1)} %collective-permute-done.2.refs_1_, f32[1,4096]{1,0:T(1,128)S(1)} %copy-done.6, ...), custom_call_target="tpu_custom_call", output_to_operand_aliasing={{0}: (8, {})} | custom-call | flops 1073741824 | bytes 16777216 | tf_op jit(solution)/shard_map/pallas_call | solution.py:232
  29.9 0.6 collective-permute-start.3
  30.5 1.2 shard_map.151.refs_0_
  31.8 1.3 %collective-permute-start.5 = (bf16[64,2048]{1,0:T(8,128)(2,1)S(1)}, bf16[64,2048]{1,0:T(8,128)(2,1)S(1)}, u32[]{:S(2)}, u32[]{:S(2)}) collective-permute-start(bf16[64,2048]{1,0:T(8,128)(2,1)S(1)} %shard_map.152), channel_id=1, source_target_pairs={{0,6},{1,7},{2,4},{3,5},{16,22},{17,23},{18,20},{19,21}} | collective-permute-start | bytes 786440 | tf_op jit(solution)/shard_map/ppermute | solution.py:454
  33.1 1.3 %collective-permute-start.4 = (bf16[64,2048]{1,0:T(8,128)(2,1)S(1)}, bf16[64,2048]{1,0:T(8,128)(2,1)S(1)}, u32[]{:S(2)}, u32[]{:S(2)}) collective-permute-start(bf16[64,2048]{1,0:T(8,128)(2,1)S(1)} %shard_map.152), channel_id=1, source_target_pairs={{0,4},{1,5},{2,6},{3,7},{16,20},{17,21},{18,22},{19,23}} | collective-permute-start | bytes 786440 | tf_op jit(solution)/shard_map/ppermute | solution.py:454
  34.4 5.3 %collective-permute-done.5.refs_1_ = bf16[64,2048]{1,0:T(8,128)(2,1)S(1)} collective-permute-done((bf16[64,2048]{1,0:T(8,128)(2,1)S(1)}, bf16[64,2048]{1,0:T(8,128)(2,1)S(1)}, u32[]{:S(2)}, u32[]{:S(2)}) %collective-permute-start.5) | collective-permute-done | bytes 262176 | tf_op jit(solution)/shard_map/ppermute | solution.py:454
  39.7 5.2 %collective-permute-done.4.refs_0_ = bf16[64,2048]{1,0:T(8,128)(2,1)S(1)} collective-permute-done((bf16[64,2048]{1,0:T(8,128)(2,1)S(1)}, bf16[64,2048]{1,0:T(8,128)(2,1)S(1)}, u32[]{:S(2)}, u32[]{:S(2)}) %collective-permute-start.4) | collective-permute-done | bytes 262176 | tf_op jit(solution)/shard_map/ppermute | solution.py:454
  45.1 1.5 %collective-permute-done.6.refs_0_ = bf16[64,2048]{1,0:T(8,128)(2,1)S(1)} collective-permute-done((bf16[64,2048]{1,0:T(8,128)(2,1)S(1)}, bf16[64,2048]{1,0:T(8,128)(2,1)S(1)}, u32[]{:S(2)}, u32[]{:S(2)}) %collective-permute-start.6) | collective-permute-done | bytes 262176 | tf_op jit(solution)/shard_map/ppermute | solution.py:345
  46.6 0.1 collective-permute-start.7
  46.8 1.4 %collective-permute-done.7.refs_1_ = bf16[64,2048]{1,0:T(8,128)(2,1)S(1)} collective-permute-done((bf16[64,2048]{1,0:T(8,128)(2,1)S(1)}, bf16[64,2048]{1,0:T(8,128)(2,1)S(1)}, u32[]{:S(2)}, u32[]{:S(2)}) %collective-permute-start.7) | collective-permute-done | bytes 262176 | tf_op jit(solution)/shard_map/ppermute | solution.py:345
  48.2 0.7 collective-permute-start.9
  48.9 0.7 collective-permute-start.8
  49.7 0.2 collective-permute-start.10
  49.9 1.4 %collective-permute-done.10.refs_0_ = bf16[64,2048]{1,0:T(8,128)(2,1)S(1)} collective-permute-done((bf16[64,2048]{1,0:T(8,128)(2,1)S(1)}, bf16[64,2048]{1,0:T(8,128)(2,1)S(1)}, u32[]{:S(2)}, u32[]{:S(2)}) %collective-permute-start.10) | collective-permute-done | bytes 262176 | tf_op jit(solution)/shard_map/ppermute | solution.py:345
  51.3 0.1 collective-permute-start.11
  51.4 1.4 %collective-permute-done.11.refs_1_ = bf16[64,2048]{1,0:T(8,128)(2,1)S(1)} collective-permute-done((bf16[64,2048]{1,0:T(8,128)(2,1)S(1)}, bf16[64,2048]{1,0:T(8,128)(2,1)S(1)}, u32[]{:S(2)}, u32[]{:S(2)}) %collective-permute-start.11) | collective-permute-done | bytes 262176 | tf_op jit(solution)/shard_map/ppermute | solution.py:345
  52.9 0.7 collective-permute-start.13
  53.6 0.7 collective-permute-start.12
  54.3 0.2 collective-permute-start.14
  54.6 1.4 %collective-permute-done.14.refs_0_ = bf16[64,2048]{1,0:T(8,128)(2,1)S(1)} collective-permute-done((bf16[64,2048]{1,0:T(8,128)(2,1)S(1)}, bf16[64,2048]{1,0:T(8,128)(2,1)S(1)}, u32[]{:S(2)}, u32[]{:S(2)}) %collective-permute-start.14) | collective-permute-done | bytes 262176 | tf_op jit(solution)/shard_map/ppermute | solution.py:345
  56.1 1.4 %collective-permute-done.15.facing = bf16[64,2048]{1,0:T(8,128)(2,1)S(1)} collective-permute-done((bf16[64,2048]{1,0:T(8,128)(2,1)S(1)}, bf16[64,2048]{1,0:T(8,128)(2,1)S(1)}, u32[]{:S(2)}, u32[]{:S(2)}) %collective-permute-start.15) | collective-permute-done | bytes 262176 | tf_op jit(solution)/shard_map/ppermute | solution.py:345
  57.5 1.3 %collective-permute-start.16 = (bf16[16,2048]{1,0:T(8,128)(2,1)S(1)}, bf16[16,2048]{1,0:T(8,128)(2,1)S(1)}, u32[]{:S(2)}, u32[]{:S(2)}) collective-permute-start(bf16[16,2048]{1,0:T(8,128)(2,1)S(1)} %get-tuple-element.63), channel_id=1, source_target_pairs={{12,0},{13,1},{14,2},{15,3},{28,16},{29,17},{30,18},{31,19}} | collective-permute-start | bytes 196616 | tf_op jit(solution)/shard_map/ppermute | solution.py:462
  58.8 0.7 collective-permute-start.17
  59.5 0.7 collective-permute-start.18
  60.2 1.4 %shard_map.168 = (f32[6,32,1024]{2,1,0:T(8,128)}, f32[32,8,1024]{2,1,0:T(8,128)}, f32[8,128]{1,0:T(8,128)S(1)}) custom-call(f32[64,1024]{1,0:T(8,128)S(1)} %get-tuple-element.66.product, f32[6,32,1024]{2,1,0:T(8,128)S(1)} %bitcast.17, f32[32,8,1024]{2,1,0:T(8,128)S(1)} %bitcast.15, f32[8,1024]{1,0:T(8,128)S(1)} %bitcast.19), custom_call_target="tpu_custom_call" | custom-call | bytes 3670016 | tf_op jit(solution)/shard_map/pallas_call | solution.py:232
  61.6 47.2 %collective-permute-done.16.refs_0_ = bf16[16,2048]{1,0:T(8,128)(2,1)S(1)} collective-permute-done((bf16[16,2048]{1,0:T(8,128)(2,1)S(1)}, bf16[16,2048]{1,0:T(8,128)(2,1)S(1)}, u32[]{:S(2)}, u32[]{:S(2)}) %collective-permute-start.16) | collective-permute-done | bytes 65568 | tf_op jit(solution)/shard_map/ppermute | solution.py:462
  108.8 1.8 %collective-permute-start.19 = (bf16[16,2048]{1,0:T(8,128)(2,1)S(1)}, bf16[16,2048]{1,0:T(8,128)(2,1)S(1)}, u32[]{:S(2)}, u32[]{:S(2)}) collective-permute-start(bf16[16,2048]{1,0:T(8,128)(2,1)S(1)} %shard_map.169.refs_0_), channel_id=1, source_target_pairs={{0,2},{1,3},{2,0},{3,1},{4,6},{5,7},{6,4},{7,5},{8,10},{9,11},{10,... | collective-permute-start | bytes 196616 | tf_op jit(solution)/shard_map/ppermute | solution.py:350
  110.6 2.5 %collective-permute-done.19.refs_1_ = bf16[16,2048]{1,0:T(8,128)(2,1)S(1)} collective-permute-done((bf16[16,2048]{1,0:T(8,128)(2,1)S(1)}, bf16[16,2048]{1,0:T(8,128)(2,1)S(1)}, u32[]{:S(2)}, u32[]{:S(2)}) %collective-permute-start.19) | collective-permute-done | bytes 65568 | tf_op jit(solution)/shard_map/ppermute | solution.py:350
  113.2 1.2 %collective-permute-done.20.other = bf16[16,2048]{1,0:T(8,128)(2,1)S(1)} collective-permute-done((bf16[16,2048]{1,0:T(8,128)(2,1)S(1)}, bf16[16,2048]{1,0:T(8,128)(2,1)S(1)}, u32[]{:S(2)}, u32[]{:S(2)}) %collective-permute-start.20) | collective-permute-done | bytes 65568 | tf_op jit(solution)/shard_map/ppermute | solution.py:345
  114.5 1.5 %shard_map.171 = (f32[2,8,128]{2,1,0:T(8,128)}, f32[16,128]{1,0:T(8,128)S(1)}) custom-call(bf16[16,2048]{1,0:T(8,128)(2,1)S(1)} %shard_map.170.own, bf16[16,2048]{1,0:T(8,128)(2,1)S(1)} %collective-permute-done.20.other, f32[1,4096]{1,0:T(1,128)S(1)} %bitcast.22, bf16[4096,128]{1,0:T(8,128)(2,1)S(1)} %copy-done.5, s32[3,32]{1,0:T(4,128)S(1)} %copy-done.13), custom_call_target="tpu_custom_call" | custom-call | flops 16777216 | bytes 1048576 | tf_op jit(solution)/shard_map/pallas_call | solution.py:232
  116.0 1.5 %collective-permute-start.23 = (f32[16,128]{1,0:T(8,128)S(1)}, f32[16,128]{1,0:T(8,128)S(1)}, u32[]{:S(2)}, u32[]{:S(2)}) collective-permute-start(f32[16,128]{1,0:T(8,128)S(1)} %get-tuple-element.69.refs_0_), channel_id=1, source_target_pairs={{0,3},{1,0},{2,1},{3,2},{4,7},{5,4},{6,5},{7,6},{8,11},{9,8},{10,9... | collective-permute-start | bytes 24584 | tf_op jit(solution)/shard_map/ppermute | solution.py:488
  117.5 0.3 collective-permute-start.22
  117.8 0.2 collective-permute-start.21
  118.0 0.9 collective-permute-done.23.refs_3_
  118.9 2.3 %collective-permute-done.22.refs_2_ = f32[16,128]{1,0:T(8,128)S(1)} collective-permute-done((f32[16,128]{1,0:T(8,128)S(1)}, f32[16,128]{1,0:T(8,128)S(1)}, u32[]{:S(2)}, u32[]{:S(2)}) %collective-permute-start.22) | collective-permute-done | bytes 8224 | tf_op jit(solution)/shard_map/ppermute | solution.py:488
  121.2 0.7 shard_map.172
  (54 shorter events, 0.8 us)
Async XLA Ops:
  0.6 1.2 %copy-start.4 = (bf16[512,1024]{1,0:T(8,128)(2,1)S(1)}, bf16[512,1024]{1,0:T(8,128)(2,1)}, u32[]{:S(2)}) copy-start(bf16[512,1024]{1,0:T(8,128)(2,1)} %embedding.1) | copy-start | bytes 3145732
  1.9 0.7 copy-start.12
  2.5 19.9 %copy-start.6 = (f32[1,4096]{1,0:T(1,128)S(1)}, f32[1,4096]{1,0:T(1,128)}, u32[]{:S(2)}) copy-start(f32[1,4096]{1,0:T(1,128)} %refs_1_.11) | copy-start | bytes 49156
  3.0 6.5 %collective-permute-start = (bf16[64,1024]{1,0:T(8,128)(2,1)S(1)}, bf16[64,1024]{1,0:T(8,128)(2,1)S(1)}, u32[]{:S(2)}, u32[]{:S(2)}) collective-permute-start(bf16[64,1024]{1,0:T(8,128)(2,1)S(1)} %shard_map.147.refs_0_), channel_id=1, source_target_pairs={{0,2},{1,3},{2,0},{3,1},{4,6},{5,7},{6,4},{7,5},{8,10},{9,11},{10,... | collective-permute-start | bytes 393224 | tf_op jit(solution)/shard_map/ppermute | solution.py:350
  6.0 20.0 %collective-permute-start.1 = (bf16[64,1024]{1,0:T(8,128)(2,1)S(1)}, bf16[64,1024]{1,0:T(8,128)(2,1)S(1)}, u32[]{:S(2)}, u32[]{:S(2)}) collective-permute-start(bf16[64,1024]{1,0:T(8,128)(2,1)S(1)} %shard_map.147.refs_0_), channel_id=1, source_target_pairs={{0,1},{1,0},{2,3},{3,2},{4,5},{5,4},{6,7},{7,6},{8,9},{9,8},{10,11... | collective-permute-start | bytes 393224 | tf_op jit(solution)/shard_map/ppermute | solution.py:345
  9.5 16.5 %collective-permute-start.2 = (bf16[64,1024]{1,0:T(8,128)(2,1)S(1)}, bf16[64,1024]{1,0:T(8,128)(2,1)S(1)}, u32[]{:S(2)}, u32[]{:S(2)}) collective-permute-start(bf16[64,1024]{1,0:T(8,128)(2,1)S(1)} %collective-permute-done.refs_1_), channel_id=1, source_target_pairs={{0,1},{1,0},{2,3},{3,2},{4,5},{5,4},{6,7},{7,6},{8,9},{9,8},{10,11... | collective-permute-start | bytes 393224 | tf_op jit(solution)/shard_map/ppermute | solution.py:345
  9.5 1.2 %copy-start = (f32[1,32,8,1024]{3,2,1,0:T(8,128)S(1)}, f32[1,32,8,1024]{3,2,1,0:T(8,128)}, u32[]{:S(2)}) copy-start(f32[1,32,8,1024]{3,2,1,0:T(8,128)} %param.21) | copy-start | bytes 3145732
  10.8 1.1 copy-start.2
  11.9 0.8 copy-start.7
  12.6 0.8 copy-start.9
  13.4 0.7 copy-start.10
  29.9 1.8 %collective-permute-start.3 = (bf16[64,2048]{1,0:T(8,128)(2,1)S(1)}, bf16[64,2048]{1,0:T(8,128)(2,1)S(1)}, u32[]{:S(2)}, u32[]{:S(2)}) collective-permute-start(bf16[64,2048]{1,0:T(8,128)(2,1)S(1)} %get-tuple-element.46), channel_id=1, source_target_pairs={{0,1},{1,0},{2,3},{3,2},{4,5},{5,4},{6,7},{7,6},{8,9},{9,8},{10,11... | collective-permute-start | bytes 786440 | tf_op jit(solution)/shard_map/ppermute | solution.py:345
  31.8 8.0 %collective-permute-start.5 = (bf16[64,2048]{1,0:T(8,128)(2,1)S(1)}, bf16[64,2048]{1,0:T(8,128)(2,1)S(1)}, u32[]{:S(2)}, u32[]{:S(2)}) collective-permute-start(bf16[64,2048]{1,0:T(8,128)(2,1)S(1)} %shard_map.152), channel_id=1, source_target_pairs={{0,6},{1,7},{2,4},{3,5},{16,22},{17,23},{18,20},{19,21}} | collective-permute-start | bytes 786440 | tf_op jit(solution)/shard_map/ppermute | solution.py:454
  33.1 11.9 %collective-permute-start.4 = (bf16[64,2048]{1,0:T(8,128)(2,1)S(1)}, bf16[64,2048]{1,0:T(8,128)(2,1)S(1)}, u32[]{:S(2)}, u32[]{:S(2)}) collective-permute-start(bf16[64,2048]{1,0:T(8,128)(2,1)S(1)} %shard_map.152), channel_id=1, source_target_pairs={{0,4},{1,5},{2,6},{3,7},{16,20},{17,21},{18,22},{19,23}} | collective-permute-start | bytes 786440 | tf_op jit(solution)/shard_map/ppermute | solution.py:454
  45.0 1.6 %collective-permute-start.6 = (bf16[64,2048]{1,0:T(8,128)(2,1)S(1)}, bf16[64,2048]{1,0:T(8,128)(2,1)S(1)}, u32[]{:S(2)}, u32[]{:S(2)}) collective-permute-start(bf16[64,2048]{1,0:T(8,128)(2,1)S(1)} %shard_map.153.refs_0_), channel_id=1, source_target_pairs={{0,1},{1,0},{2,3},{3,2},{4,5},{5,4},{6,7},{7,6},{8,9},{9,8},{10,11... | collective-permute-start | bytes 786440 | tf_op jit(solution)/shard_map/ppermute | solution.py:345
  46.6 1.5 %collective-permute-start.7 = (bf16[64,2048]{1,0:T(8,128)(2,1)S(1)}, bf16[64,2048]{1,0:T(8,128)(2,1)S(1)}, u32[]{:S(2)}, u32[]{:S(2)}) collective-permute-start(bf16[64,2048]{1,0:T(8,128)(2,1)S(1)} %get-tuple-element.51), channel_id=1, source_target_pairs={{0,1},{1,0},{2,3},{3,2},{4,5},{5,4},{6,7},{7,6},{8,9},{9,8},{10,11... | collective-permute-start | bytes 786440 | tf_op jit(solution)/shard_map/ppermute | solution.py:345
  48.2 1.4 %collective-permute-start.9 = (bf16[64,2048]{1,0:T(8,128)(2,1)S(1)}, bf16[64,2048]{1,0:T(8,128)(2,1)S(1)}, u32[]{:S(2)}, u32[]{:S(2)}) collective-permute-start(bf16[64,2048]{1,0:T(8,128)(2,1)S(1)} %shard_map.157), channel_id=1, source_target_pairs={{4,10},{5,11},{6,8},{7,9},{20,26},{21,27},{22,24},{23,25}} | collective-permute-start | bytes 786440 | tf_op jit(solution)/shard_map/ppermute | solution.py:454
  48.9 0.7 collective-permute-start.8
  49.7 1.6 %collective-permute-start.10 = (bf16[64,2048]{1,0:T(8,128)(2,1)S(1)}, bf16[64,2048]{1,0:T(8,128)(2,1)S(1)}, u32[]{:S(2)}, u32[]{:S(2)}) collective-permute-start(bf16[64,2048]{1,0:T(8,128)(2,1)S(1)} %shard_map.158.refs_0_), channel_id=1, source_target_pairs={{0,1},{1,0},{2,3},{3,2},{4,5},{5,4},{6,7},{7,6},{8,9},{9,8},{10,11... | collective-permute-start | bytes 786440 | tf_op jit(solution)/shard_map/ppermute | solution.py:345
  51.3 1.5 %collective-permute-start.11 = (bf16[64,2048]{1,0:T(8,128)(2,1)S(1)}, bf16[64,2048]{1,0:T(8,128)(2,1)S(1)}, u32[]{:S(2)}, u32[]{:S(2)}) collective-permute-start(bf16[64,2048]{1,0:T(8,128)(2,1)S(1)} %get-tuple-element.56), channel_id=1, source_target_pairs={{0,1},{1,0},{2,3},{3,2},{4,5},{5,4},{6,7},{7,6},{8,9},{9,8},{10,11... | collective-permute-start | bytes 786440 | tf_op jit(solution)/shard_map/ppermute | solution.py:345
  52.9 1.4 %collective-permute-start.13 = (bf16[64,2048]{1,0:T(8,128)(2,1)S(1)}, bf16[64,2048]{1,0:T(8,128)(2,1)S(1)}, u32[]{:S(2)}, u32[]{:S(2)}) collective-permute-start(bf16[64,2048]{1,0:T(8,128)(2,1)S(1)} %shard_map.162), channel_id=1, source_target_pairs={{8,14},{9,15},{10,12},{11,13},{24,30},{25,31},{26,28},{27,29}} | collective-permute-start | bytes 786440 | tf_op jit(solution)/shard_map/ppermute | solution.py:454
  53.6 0.7 collective-permute-start.12
  54.3 1.6 %collective-permute-start.14 = (bf16[64,2048]{1,0:T(8,128)(2,1)S(1)}, bf16[64,2048]{1,0:T(8,128)(2,1)S(1)}, u32[]{:S(2)}, u32[]{:S(2)}) collective-permute-start(bf16[64,2048]{1,0:T(8,128)(2,1)S(1)} %shard_map.163.refs_0_), channel_id=1, source_target_pairs={{0,1},{1,0},{2,3},{3,2},{4,5},{5,4},{6,7},{7,6},{8,9},{9,8},{10,11... | collective-permute-start | bytes 786440 | tf_op jit(solution)/shard_map/ppermute | solution.py:345
  54.5 5.6 %copy-start.1 = (f32[1,32,8,1024]{3,2,1,0:T(8,128)S(1)}, f32[1,32,8,1024]{3,2,1,0:T(8,128)}, u32[]{:S(2)}) copy-start(f32[1,32,8,1024]{3,2,1,0:T(8,128)} %param.21) | copy-start | bytes 3145732
  54.5 5.6 %copy-start.3 = (f32[1,32,6,1024]{3,1,2,0:T(8,128)S(1)}, f32[1,32,6,1024]{3,1,2,0:T(8,128)}, u32[]{:S(2)}) copy-start(f32[1,32,6,1024]{3,1,2,0:T(8,128)} %param.20) | copy-start | bytes 2359300
  54.5 5.6 %copy-start.8 = (f32[1,8,1024]{2,1,0:T(8,128)S(1)}, f32[1,8,1024]{2,1,0:T(8,128)}, u32[]{:S(2)}) copy-start(f32[1,8,1024]{2,1,0:T(8,128)} %param.18) | copy-start | bytes 98308
  54.5 59.9 %copy-start.5 = (bf16[4096,128]{1,0:T(8,128)(2,1)S(1)}, bf16[4096,128]{1,0:T(8,128)(2,1)}, u32[]{:S(2)}) copy-start(bf16[4096,128]{1,0:T(8,128)(2,1)} %unembed.1) | copy-start | bytes 3145732
  54.6 59.9 %copy-start.11 = (f32[4096]{0:T(1024)S(1)}, f32[4096]{0:T(1024)}, u32[]{:S(2)}) copy-start(f32[4096]{0:T(1024)} %param.22) | copy-start | bytes 49156
  54.6 59.9 %copy-start.13 = (s32[3,32]{1,0:T(4,128)S(1)}, s32[3,32]{1,0:T(4,128)}, u32[]{:S(2)}) copy-start(s32[3,32]{1,0:T(4,128)} %tokens.3) | copy-start | bytes 1156
  55.9 1.5 %collective-permute-start.15 = (bf16[64,2048]{1,0:T(8,128)(2,1)S(1)}, bf16[64,2048]{1,0:T(8,128)(2,1)S(1)}, u32[]{:S(2)}, u32[]{:S(2)}) collective-permute-start(bf16[64,2048]{1,0:T(8,128)(2,1)S(1)} %get-tuple-element.61), channel_id=1, source_target_pairs={{0,1},{1,0},{2,3},{3,2},{4,5},{5,4},{6,7},{7,6},{8,9},{9,8},{10,11... | collective-permute-start | bytes 786440 | tf_op jit(solution)/shard_map/ppermute | solution.py:345
  57.5 51.2 %collective-permute-start.16 = (bf16[16,2048]{1,0:T(8,128)(2,1)S(1)}, bf16[16,2048]{1,0:T(8,128)(2,1)S(1)}, u32[]{:S(2)}, u32[]{:S(2)}) collective-permute-start(bf16[16,2048]{1,0:T(8,128)(2,1)S(1)} %get-tuple-element.63), channel_id=1, source_target_pairs={{12,0},{13,1},{14,2},{15,3},{28,16},{29,17},{30,18},{31,19}} | collective-permute-start | bytes 196616 | tf_op jit(solution)/shard_map/ppermute | solution.py:462
  58.8 49.9 %collective-permute-start.17 = (bf16[16,2048]{1,0:T(8,128)(2,1)S(1)}, bf16[16,2048]{1,0:T(8,128)(2,1)S(1)}, u32[]{:S(2)}, u32[]{:S(2)}) collective-permute-start(bf16[16,2048]{1,0:T(8,128)(2,1)S(1)} %get-tuple-element.64), channel_id=1, source_target_pairs={{12,4},{13,5},{14,6},{15,7},{28,20},{29,21},{30,22},{31,23}} | collective-permute-start | bytes 196616 | tf_op jit(solution)/shard_map/ppermute | solution.py:462
  59.5 49.3 %collective-permute-start.18 = (bf16[16,2048]{1,0:T(8,128)(2,1)S(1)}, bf16[16,2048]{1,0:T(8,128)(2,1)S(1)}, u32[]{:S(2)}, u32[]{:S(2)}) collective-permute-start(bf16[16,2048]{1,0:T(8,128)(2,1)S(1)} %get-tuple-element.65), channel_id=1, source_target_pairs={{12,8},{13,9},{14,10},{15,11},{28,24},{29,25},{30,26},{31,27}} | collective-permute-start | bytes 196616 | tf_op jit(solution)/shard_map/ppermute | solution.py:462
  108.8 4.3 %collective-permute-start.19 = (bf16[16,2048]{1,0:T(8,128)(2,1)S(1)}, bf16[16,2048]{1,0:T(8,128)(2,1)S(1)}, u32[]{:S(2)}, u32[]{:S(2)}) collective-permute-start(bf16[16,2048]{1,0:T(8,128)(2,1)S(1)} %shard_map.169.refs_0_), channel_id=1, source_target_pairs={{0,2},{1,3},{2,0},{3,1},{4,6},{5,7},{6,4},{7,5},{8,10},{9,11},{10,... | collective-permute-start | bytes 196616 | tf_op jit(solution)/shard_map/ppermute | solution.py:350
  113.2 1.3 %collective-permute-start.20 = (bf16[16,2048]{1,0:T(8,128)(2,1)S(1)}, bf16[16,2048]{1,0:T(8,128)(2,1)S(1)}, u32[]{:S(2)}, u32[]{:S(2)}) collective-permute-start(bf16[16,2048]{1,0:T(8,128)(2,1)S(1)} %shard_map.170.own), channel_id=1, source_target_pairs={{0,1},{1,0},{2,3},{3,2},{4,5},{5,4},{6,7},{7,6},{8,9},{9,8},{10,11... | collective-permute-start | bytes 196616 | tf_op jit(solution)/shard_map/ppermute | solution.py:345
  116.0 2.9 %collective-permute-start.23 = (f32[16,128]{1,0:T(8,128)S(1)}, f32[16,128]{1,0:T(8,128)S(1)}, u32[]{:S(2)}, u32[]{:S(2)}) collective-permute-start(f32[16,128]{1,0:T(8,128)S(1)} %get-tuple-element.69.refs_0_), channel_id=1, source_target_pairs={{0,3},{1,0},{2,1},{3,2},{4,7},{5,4},{6,5},{7,6},{8,11},{9,8},{10,9... | collective-permute-start | bytes 24584 | tf_op jit(solution)/shard_map/ppermute | solution.py:488
  117.5 3.7 %collective-permute-start.22 = (f32[16,128]{1,0:T(8,128)S(1)}, f32[16,128]{1,0:T(8,128)S(1)}, u32[]{:S(2)}, u32[]{:S(2)}) collective-permute-start(f32[16,128]{1,0:T(8,128)S(1)} %get-tuple-element.69.refs_0_), channel_id=1, source_target_pairs={{0,2},{1,3},{2,0},{3,1},{4,6},{5,7},{6,4},{7,5},{8,10},{9,11},{10,... | collective-permute-start | bytes 24584 | tf_op jit(solution)/shard_map/ppermute | solution.py:488
  117.8 3.4 %collective-permute-start.21 = (f32[16,128]{1,0:T(8,128)S(1)}, f32[16,128]{1,0:T(8,128)S(1)}, u32[]{:S(2)}, u32[]{:S(2)}) collective-permute-start(f32[16,128]{1,0:T(8,128)S(1)} %get-tuple-element.69.refs_0_), channel_id=1, source_target_pairs={{0,1},{1,2},{2,3},{3,0},{4,5},{5,6},{6,7},{7,4},{8,9},{9,10},{10,1... | collective-permute-start | bytes 24584 | tf_op jit(solution)/shard_map/ppermute | solution.py:488
